TPU v7x, 32 devices: a whole 2x2x4 slice. The times are simulated.
32 devices in a mesh: row: 4 (over y, x), col: 8 (over z, core).
Axes of the slice: x: 2, y: 2, z: 4, core: 2. Of those that a mesh axis runs over, the one named last changes fastest.
Arguments:
- boundary_start: float32 [16384, 128], P('row'), may hold values from -6 to 6
- volume_start: float32 [256, 512, 128], P(('row', 'col')), may hold values from -6 to 6
- diag_part: float32 [16384], P(('row', 'col')), may hold values from 1 to 2
- incident: float32 [16384, 128], P(('row', 'col')), may hold values from -6 to 6
- kernel: float32 [16384, 16384], P('row', 'col'), may hold values from -0.015625 to 0.015625
- elem_mats: float32 [256, 512, 512], P(('row', 'col')), may hold values from -0.078125 to 0.078125
- trace_owner: int32 [16384, 1], replicated, may hold values from 0 to 31; in each aligned block of 512 rows (0 to 511, 512 to 1023, ...) at most 32 rows name the same one
- trace_slot: int32 [16384], replicated, may hold values from 0 to 4095
- return_owner: int32 [16384, 1], replicated, may hold values from 0 to 31; in each aligned block of 512 rows (0 to 511, 512 to 1023, ...) at most 32 rows name the same one
- return_slot: int32 [16384], replicated, may hold values from 0 to 4095
- face_match: int32 [256, 64], P(('row', 'col')), may hold values from 0 to 63, each once within a row
Outputs:
- boundary_final: float32 [16384, 128], P('row')
- volume_final: float32 [256, 512, 128], P(('row', 'col'))
Inputs may be any that keep to these rules, and one draw needn't show every extreme that they name: `trace_owner`: in each aligned block of 512 boundary rows (the rows of one device), no device is named more than 32 times; some device is named exactly 32 times in some block. `return_owner`: in each aligned block of 512 boundary rows (the rows of one device), no device is named more than 32 times; some device is named exactly 32 times in some block. `face_match`: each row is a permutation of 0 to 63.
All inputs are finite; a program needn't handle non-finite values.
Results may differ from a plain program's by a relative error of at most 0.0001.
Values sent between devices are 32-bit elements; how exact they have to be, the bound alone decides.
A program may use at most 128 MiB of HBM per device.

v0:
```python
import jax
import jax.numpy as jnp
from jax import lax
from jax.sharding import PartitionSpec as P

ITERS = 3


boundary_step = 0.5
volume_step = 0.6
face_weight = 0.5


def passed_along(block, axis, distance):
    devices = range(lax.axis_size(axis))
    route = [(i - distance, i) for i in devices if i - distance in devices]
    return lax.ppermute(block, axis, route)


def spread(block, axis, holder):
    block = jnp.where(lax.axis_index(axis) == holder, block, jnp.zeros_like(block))
    return lax.psum(block, axis)


def slot_rank(owners):
    row_total = owners.shape[0]
    same_owner = owners[:, None] == owners[None, :]
    positions = jnp.arange(row_total, dtype=jnp.int32)
    earlier = positions[None, :] < positions[:, None]
    return jnp.sum((same_owner & earlier).astype(jnp.int32), axis=1)


def send_plan(owners, rank_rows, devices, capacity):
    positions = jnp.arange(owners.shape[0], dtype=jnp.int32)
    targets = jnp.arange(devices, dtype=jnp.int32)
    places = jnp.arange(capacity, dtype=jnp.int32)
    select = (owners[None, None, :] == targets[:, None, None]) & (
        rank_rows[None, None, :] == places[None, :, None]
    )
    index = jnp.sum(jnp.where(select, positions[None, None, :], 0), axis=2)
    valid_slot = jnp.any(select, axis=2)
    return (index, valid_slot)


def block_plan(owner_blocks, slot_blocks, device_self, capacity):
    mine_rows = owner_blocks == device_self
    rank_rows = jnp.cumsum(mine_rows.astype(jnp.int32), axis=1) - 1
    places = jnp.arange(capacity, dtype=jnp.int32)
    select = mine_rows[:, None, :] & (rank_rows[:, None, :] == places[None, :, None])
    index = jnp.sum(jnp.where(select, slot_blocks[:, None, :], 0), axis=2)
    valid_slot = jnp.any(select, axis=2)
    return (index, valid_slot)


def shards(
    boundary_start,
    volume_start,
    diag_part,
    incident,
    kernel,
    elem_mats,
    trace_owner,
    trace_slot,
    return_owner,
    return_slot,
    face_match,
):
    highest = lax.Precision.HIGHEST
    devices = lax.axis_size(("row", "col"))
    row_devices = lax.axis_size("row")
    col_devices = lax.axis_size("col")
    device_self = lax.axis_index(("row", "col"))
    col_index = lax.axis_index("col")
    total_rows = trace_slot.shape[0]
    share_rows = total_rows // devices
    capacity = max(2, 2 * share_rows // devices)
    panel_length = total_rows // col_devices
    per_panel = col_devices // row_devices
    elem_count, node_count, columns = volume_start.shape
    face_count = face_match.shape[1]
    trace_blocks = trace_owner[:, 0].reshape(devices, share_rows)
    trace_slots = trace_slot.reshape(devices, share_rows)
    return_blocks = return_owner[:, 0].reshape(devices, share_rows)
    return_slots = return_slot.reshape(devices, share_rows)
    trace_send, trace_send_ok = block_plan(trace_blocks, trace_slots, device_self, capacity)
    own_trace = lax.dynamic_index_in_dim(trace_blocks, device_self, 0, keepdims=False)
    trace_pick = own_trace * capacity + slot_rank(own_trace)
    own_return = lax.dynamic_index_in_dim(return_blocks, device_self, 0, keepdims=False)
    flux_send, flux_send_ok = send_plan(own_return, slot_rank(own_return), devices, capacity)
    flux_take, flux_take_ok = block_plan(return_blocks, return_slots, device_self, capacity)
    panel_current = boundary_start
    volume_field = volume_start
    for sweep_index in range(ITERS):
        share_current = lax.dynamic_slice_in_dim(
            panel_current, col_index * share_rows, share_rows, 0
        )
        volume_flat = volume_field.reshape(elem_count * node_count, columns)
        outgoing = jnp.where(trace_send_ok[:, :, None], volume_flat[trace_send], 0.0)
        arrived = lax.all_to_all(outgoing, ("row", "col"), split_axis=0, concat_axis=0, tiled=True)
        traced = arrived.reshape(devices * capacity, columns)[trace_pick]
        leaving = jnp.where(flux_send_ok[:, :, None], share_current[flux_send], 0.0)
        landed = lax.all_to_all(leaving, ("row", "col"), split_axis=0, concat_axis=0, tiled=True)
        landed_rows = jnp.where(flux_take_ok[:, :, None], landed, 0.0).reshape(
            devices * capacity, columns
        )
        flux_field = (
            jnp.zeros_like(volume_flat)
            .at[flux_take.reshape(-1)]
            .add(landed_rows)
            .reshape(volume_field.shape)
        )
        lower_faces = passed_along(volume_field[:, node_count - face_count :, :], ("row", "col"), 1)
        matched = jax.vmap(lambda face_rows, face_order: face_rows[face_order])(
            lower_faces, face_match
        )
        half_panel = lax.dynamic_slice_in_dim(
            panel_current, col_index % per_panel * panel_length, panel_length, 0
        )
        column_values = spread(half_panel, "row", col_index // per_panel)
        local_term = diag_part[:, None] * share_current - incident - traced
        partial_value = jnp.dot(
            kernel, column_values, precision=highest, preferred_element_type=jnp.float32
        )
        row_start = col_index * share_rows
        own_part = lax.dynamic_slice_in_dim(partial_value, row_start, share_rows, 0) + local_term
        partial_value = lax.dynamic_update_slice_in_dim(partial_value, own_part, row_start, 0)
        residual = lax.psum(partial_value, "col")
        panel_current = panel_current - boundary_step * residual
        applied = jnp.einsum("enm,emr->enr", elem_mats, volume_field, precision=highest)
        updated = volume_field - volume_step * (volume_field + applied - flux_field)
        volume_field = updated.at[:, :face_count, :].add(volume_step * face_weight * matched)
    return (panel_current, volume_field)


def solution(mesh):
    placed = (
        P("row", None),
        P(("row", "col"), None, None),
        P(("row", "col")),
        P(("row", "col"), None),
        P("row", "col"),
        P(("row", "col"), None, None),
        P(),
        P(),
        P(),
        P(),
        P(("row", "col"), None),
    )
    return jax.shard_map(
        shards,
        mesh=mesh,
        in_specs=placed,
        out_specs=(P("row", None), P(("row", "col"), None, None)),
        check_vma=False,
    )
```

profile of v0, /device:TPU:0, one launch (start us, length us, event | category | flops | bytes accessed | tf_op | source)
XLA Modules:
  0.0 601.1 jit_solution(13699476681869330466)
XLA Ops:
  7.2 2.9 copy.59
  20.9 7.3 %all-to-all-start = ((f32[32,32,128]{2,1,0:T(8,128)}), f32[32,32,128]{2,1,0:T(8,128)S(1)}, u32[]{:S(2)}, u32[]{:S(2)}) async-start(f32[32,32,128]{2,1,0:T(8,128)} %broadcast_select_fusion.8), calls=%async_computation | async-start | bytes 1048576 | tf_op jit(solution)/shard_map/all_to_all | solution.py:99
  36.1 8.7 %all-to-all-done = f32[32,32,128]{2,1,0:T(8,128)S(1)} async-done(((f32[32,32,128]{2,1,0:T(8,128)}), f32[32,32,128]{2,1,0:T(8,128)S(1)}, u32[]{:S(2)}, u32[]{:S(2)}) %all-to-all-start) | async-done | bytes 524320 | tf_op jit(solution)/shard_map/all_to_all | solution.py:99
  46.0 23.2 %all-reduce.7.cloned.1.call-done = f32[2048,128]{0,1:T(8,128)} async-done(((f32[2048,128]{0,1:T(8,128)}), f32[2048,128]{0,1:T(8,128)}) %all-reduce.7.cloned.1.call-update) | async-done | bytes 1048592 | tf_op jit(solution)/shard_map/psum | solution.py:22
  69.2 38.4 %fusion.29 = f32[128,4096]{1,0:T(8,128)S(1)} fusion(f32[2048,128]{0,1:T(8,128)} %all-reduce.7.cloned.1.call-done, f32[4096,2048]{1,0:T(8,128)} %param.21), kind=kOutput, calls=%fused_computation.106 | convolution fusion | flops 12884901888 | bytes 36700160 | tf_op jit(solution)/shard_map/dot_general | solution.py:121
  114.6 4.6 all-to-all-start.1
  120.9 3.7 gather_fusion.9
  124.7 10.8 %all-to-all-done.1 = f32[32,32,128]{2,1,0:T(8,128)S(1)} async-done(((f32[32,32,128]{2,1,0:T(8,128)}), f32[32,32,128]{2,1,0:T(8,128)S(1)}, u32[]{:S(2)}, u32[]{:S(2)}) %all-to-all-start.1) | async-done | bytes 524320 | tf_op jit(solution)/shard_map/all_to_all | solution.py:102
  135.7 7.6 %scatter_custom_fusion = f32[4096,128]{1,0:T(8,128)} fusion(s32[1024]{0:T(1024)S(1)} %bitcast.132, f32[1024,128]{1,0:T(8,128)S(1)} %bitcast.123, f32[]{:T(128)} %constant.143.clone.1), kind=kCustom, calls=%fused_computation.44 | custom fusion | flops 131072 | bytes 2097156 | tf_op jit(solution)/shard_map/scatter-add | solution.py:109
  143.2 11.2 %multiply_subtract_fusion.2 = f32[8,512,128]{2,1,0:T(8,128)S(1)} fusion(f32[8,512,128]{2,1,0:T(8,128)} %param.18, f32[8,512,128]{2,1,0:T(8,128)} %bitcast.112, f32[8,512,512]{2,1,0:T(8,128)} %param.22), kind=kOutput, calls=%fused_computation.28 | convolution fusion | flops 3223322624 | bytes 14680064 | tf_op jit(solution)/shard_map/enm,emr->enr/dot_general | solution.py:129
  154.5 2.8 gather_fusion.3
  157.3 33.8 %all-reduce.9.cloned.1.call-done = f32[4096,128]{0,1:T(8,128)} async-done(((f32[4096,128]{0,1:T(8,128)}), f32[4096,128]{0,1:T(8,128)}) %all-reduce.9.cloned.1.call-update) | async-done | bytes 2097168 | tf_op jit(solution)/shard_map/psum | solution.py:127
  196.2 20.6 %all_to_all.30 = f32[32,32,128]{2,1,0:T(8,128)S(1)} all-to-all(f32[32,32,128]{2,1,0:T(8,128)S(1)} %broadcast_select_fusion.5), channel_id=1, replica_groups=mesh['row'=4,'col'=8] {'row','col'}, dimensions={0} | all-to-all | bytes 1048576 | tf_op jit(solution)/shard_map/all_to_all | solution.py:99
  218.0 35.8 %all-reduce.11.cloned.1.call-done = f32[2048,128]{0,1:T(8,128)} async-done(((f32[2048,128]{0,1:T(8,128)}), f32[2048,128]{0,1:T(8,128)}) %all-reduce.11.cloned.1.call-update) | async-done | bytes 1048592 | tf_op jit(solution)/shard_map/psum | solution.py:22
  253.9 39.1 %fusion.30 = f32[128,4096]{1,0:T(8,128)} fusion(f32[2048,128]{0,1:T(8,128)} %all-reduce.11.cloned.1.call-done, f32[4096,2048]{1,0:T(8,128)} %param.21), kind=kOutput, calls=%fused_computation.107 | convolution fusion | flops 12884901888 | bytes 36700160 | tf_op jit(solution)/shard_map/dot_general | solution.py:121
  297.2 2.8 gather_fusion.5
  301.0 4.6 all-to-all-start.3
  309.0 3.7 gather_fusion.10
  312.8 9.4 %all-to-all-done.3 = f32[32,32,128]{2,1,0:T(8,128)S(1)} async-done(((f32[32,32,128]{2,1,0:T(8,128)}), f32[32,32,128]{2,1,0:T(8,128)S(1)}, u32[]{:S(2)}, u32[]{:S(2)}) %all-to-all-start.3) | async-done | bytes 524320 | tf_op jit(solution)/shard_map/all_to_all | solution.py:102
  322.4 7.7 %scatter_custom_fusion.1 = f32[4096,128]{1,0:T(8,128)} fusion(s32[1024]{0:T(1024)S(1)} %bitcast.133, f32[1024,128]{1,0:T(8,128)S(1)} %bitcast.124, f32[]{:T(128)} %constant.143.clone.1), kind=kCustom, calls=%fused_computation.42 | custom fusion | flops 131072 | bytes 2097156 | tf_op jit(solution)/shard_map/scatter-add | solution.py:109
  330.1 11.0 %fusion.6 = f32[8,512,128]{2,1,0:T(8,128)S(1)} fusion(f32[8,512,128]{2,1,0:T(8,128)} %copy-done, f32[8,512,128]{2,1,0:T(8,128)} %bitcast.111, f32[8,512,512]{2,1,0:T(8,128)} %param.22), kind=kOutput, calls=%fused_computation.25 | convolution fusion | flops 3223322624 | bytes 14680064 | tf_op jit(solution)/shard_map/enm,emr->enr/dot_general | solution.py:129
  344.0 46.5 %all-reduce.13.cloned.1.call-done = f32[4096,128]{0,1:T(8,128)} async-done(((f32[4096,128]{0,1:T(8,128)}), f32[4096,128]{0,1:T(8,128)}) %all-reduce.13.cloned.1.call-update) | async-done | bytes 2097168 | tf_op jit(solution)/shard_map/psum | solution.py:127
  395.6 20.3 %all_to_all.31 = f32[32,32,128]{2,1,0:T(8,128)S(1)} all-to-all(f32[32,32,128]{2,1,0:T(8,128)S(1)} %broadcast_select_fusion.2), channel_id=1, replica_groups=mesh['row'=4,'col'=8] {'row','col'}, dimensions={0} | all-to-all | bytes 1048576 | tf_op jit(solution)/shard_map/all_to_all | solution.py:99
  417.0 36.1 %all-reduce.15.cloned.1.call-done = f32[2048,128]{0,1:T(8,128)} async-done(((f32[2048,128]{0,1:T(8,128)}), f32[2048,128]{0,1:T(8,128)}) %all-reduce.15.cloned.1.call-update) | async-done | bytes 1048592 | tf_op jit(solution)/shard_map/psum | solution.py:22
  453.1 39.1 %fusion.31 = f32[128,4096]{1,0:T(8,128)} fusion(f32[2048,128]{0,1:T(8,128)} %all-reduce.15.cloned.1.call-done, f32[4096,2048]{1,0:T(8,128)} %param.21), kind=kOutput, calls=%fused_computation.108 | convolution fusion | flops 12884901888 | bytes 36700160 | tf_op jit(solution)/shard_map/dot_general | solution.py:121
  496.4 2.8 gather_fusion.8
  500.2 4.6 all-to-all-start.5
  508.2 3.7 gather_fusion.11
  511.9 9.5 %all-to-all-done.5 = f32[32,32,128]{2,1,0:T(8,128)S(1)} async-done(((f32[32,32,128]{2,1,0:T(8,128)}), f32[32,32,128]{2,1,0:T(8,128)S(1)}, u32[]{:S(2)}, u32[]{:S(2)}) %all-to-all-start.5) | async-done | bytes 524320 | tf_op jit(solution)/shard_map/all_to_all | solution.py:102
  521.6 7.7 %scatter_custom_fusion.2 = f32[4096,128]{1,0:T(8,128)} fusion(s32[1024]{0:T(1024)S(1)} %bitcast.134, f32[1024,128]{1,0:T(8,128)S(1)} %bitcast.122, f32[]{:T(128)} %constant.143.clone.1), kind=kCustom, calls=%fused_computation.40 | custom fusion | flops 131072 | bytes 2097156 | tf_op jit(solution)/shard_map/scatter-add | solution.py:109
  529.3 10.8 %fusion.3 = f32[8,512,128]{2,1,0:T(8,128)} fusion(f32[8,512,128]{2,1,0:T(8,128)S(1)} %fusion.20, f32[8,512,128]{2,1,0:T(8,128)} %bitcast.110, f32[8,512,512]{2,1,0:T(8,128)} %param.22), kind=kOutput, calls=%fused_computation.21 | convolution fusion | flops 3223322624 | bytes 14680064 | tf_op jit(solution)/shard_map/enm,emr->enr/dot_general | solution.py:129
  541.8 47.9 %all-reduce.17.cloned.1.call-done = f32[4096,128]{0,1:T(8,128)} async-done(((f32[4096,128]{0,1:T(8,128)}), f32[4096,128]{0,1:T(8,128)}) %all-reduce.17.cloned.1.call-update) | async-done | bytes 2097168 | tf_op jit(solution)/shard_map/psum | solution.py:127
  (135 shorter events, 67.3 us)
Async XLA Ops:
  7.2 62.0 %all-reduce.7.cloned.1.call-start = ((), (), s32[]{:S(2)}) async-start(), calls=%async_computation.6 | async-start | bytes 2097152 | tf_op jit(solution)/shard_map/psum | solution.py:22
  10.1 2.5 copy-start.8
  10.1 2.5 copy-start.9
  10.1 5.5 copy-start.10
  10.1 6.9 %copy-start.1 = (f32[8,512,128]{2,1,0:T(8,128)S(1)}, f32[8,512,128]{2,1,0:T(8,128)}, u32[]{:S(2)}) copy-start(f32[8,512,128]{2,1,0:T(8,128)} %param.18) | copy-start | bytes 6291460
  19.8 13.8 %copy-start.7 = (f32[512,128]{1,0:T(8,128)S(1)}, f32[512,128]{1,0:T(8,128)}, u32[]{:S(2)}) copy-start(f32[512,128]{1,0:T(8,128)} %param.20) | copy-start | bytes 786436
  19.8 15.4 %copy-start.11 = (s32[16384]{0:T(1024)S(1)}, s32[16384]{0:T(1024)}, u32[]{:S(2)}) copy-start(s32[16384]{0:T(1024)} %param.26) | copy-start | bytes 196612
  20.9 23.9 %all-to-all-start = ((f32[32,32,128]{2,1,0:T(8,128)}), f32[32,32,128]{2,1,0:T(8,128)S(1)}, u32[]{:S(2)}, u32[]{:S(2)}) async-start(f32[32,32,128]{2,1,0:T(8,128)} %broadcast_select_fusion.8), calls=%async_computation | async-start | bytes 1048576 | tf_op jit(solution)/shard_map/all_to_all | solution.py:99
  28.9 92.0 %collective-permute-start = (f32[8,64,128]{2,1,0:T(8,128)}, f32[8,64,128]{2,1,0:T(8,128)S(1)}, u32[]{:S(2)}, u32[]{:S(2)}) collective-permute-start(f32[8,64,128]{2,1,0:T(8,128)} %slice.98), channel_id=1, source_target_pairs={{0,1},{1,2},{2,3},{3,4},{4,5},{5,6},{6,7},{7,8},{8,9},{9,10},{10,1... | collective-permute-start | bytes 786440 | tf_op jit(solution)/shard_map/ppermute | solution.py:17
  107.6 0.7 copy-start.12
  109.3 1.3 copy-start.5
  113.6 6.5 %copy-start.13 = (s32[8,64]{1,0:T(8,128)S(1)}, s32[8,64]{1,0:T(8,128)}, u32[]{:S(2)}) copy-start(s32[8,64]{1,0:T(8,128)} %param.27) | copy-start | bytes 6148
  114.6 20.9 %all-to-all-start.1 = ((f32[32,32,128]{2,1,0:T(8,128)}), f32[32,32,128]{2,1,0:T(8,128)S(1)}, u32[]{:S(2)}, u32[]{:S(2)}) async-start(f32[32,32,128]{2,1,0:T(8,128)} %broadcast_select_fusion.7), calls=%async_computation.1 | async-start | bytes 1048576 | tf_op jit(solution)/shard_map/all_to_all | solution.py:102
  119.2 72.0 %all-reduce.9.cloned.1.call-start = ((), (), s32[]{:S(2)}) async-start(), calls=%async_computation.7 | async-start | bytes 4194304 | tf_op jit(solution)/shard_map/psum | solution.py:127
  124.6 129.2 %all-reduce.11.cloned.1.call-start = ((), (), s32[]{:S(2)}) async-start(), calls=%async_computation.8 | async-start | bytes 2097152 | tf_op jit(solution)/shard_map/psum | solution.py:22
  154.5 151.2 %copy-start = (f32[8,512,128]{2,1,0:T(8,128)}, f32[8,512,128]{2,1,0:T(8,128)S(1)}, u32[]{:S(2)}) copy-start(f32[8,512,128]{2,1,0:T(8,128)S(1)} %fusion.21) | copy-start | bytes 6291460
  193.6 1.3 copy-start.3
  295.7 1.3 copy-start.6
  301.0 21.2 %all-to-all-start.3 = ((f32[32,32,128]{2,1,0:T(8,128)}), f32[32,32,128]{2,1,0:T(8,128)S(1)}, u32[]{:S(2)}, u32[]{:S(2)}) async-start(f32[32,32,128]{2,1,0:T(8,128)} %broadcast_select_fusion.4), calls=%async_computation.3 | async-start | bytes 1048576 | tf_op jit(solution)/shard_map/all_to_all | solution.py:102
  305.6 84.9 %all-reduce.13.cloned.1.call-start = ((), (), s32[]{:S(2)}) async-start(), calls=%async_computation.9 | async-start | bytes 4194304 | tf_op jit(solution)/shard_map/psum | solution.py:127
  305.7 3.3 collective-permute-start.1
  312.7 140.4 %all-reduce.15.cloned.1.call-start = ((), (), s32[]{:S(2)}) async-start(), calls=%async_computation.10 | async-start | bytes 2097152 | tf_op jit(solution)/shard_map/psum | solution.py:22
  393.0 1.3 copy-start.2
  495.0 1.3 copy-start.4
  500.2 21.2 %all-to-all-start.5 = ((f32[32,32,128]{2,1,0:T(8,128)}), f32[32,32,128]{2,1,0:T(8,128)S(1)}, u32[]{:S(2)}, u32[]{:S(2)}) async-start(f32[32,32,128]{2,1,0:T(8,128)} %broadcast_select_fusion.1), calls=%async_computation.5 | async-start | bytes 1048576 | tf_op jit(solution)/shard_map/all_to_all | solution.py:102
  504.8 84.9 %all-reduce.17.cloned.1.call-start = ((), (), s32[]{:S(2)}) async-start(), calls=%async_computation.11 | async-start | bytes 4194304 | tf_op jit(solution)/shard_map/psum | solution.py:127
  504.9 3.3 collective-permute-start.2
Sparse Core Ops, SparseCore 0:
  12.7 56.4 all-reduce.6
  124.7 66.3 all-reduce.8
  196.1 57.6 all-reduce.10
  312.9 77.6 all-reduce.12
  395.5 57.5 all-reduce.14
  512.0 77.6 all-reduce.16
where the time goes:
time: 605 us; the launch traced here: 601 us
  waiting for transfers between devices  264 us (44%)
  matrix products  150 us (25%)
  other arithmetic  53.7 us (9%)
  local copies, waits for them, and re-layouts  49 us (8%)
  blocking collectives  40.9 us (7%)
  starting transfers between devices  28.6 us (5%)
  between operations  15.1 us (2%)
    psum x3, waiting for transfers between devices, shards(): residual = lax.psum(partial_value, 'col')  128 us
    dot_general x3, matrix products, shards(): jnp.dot(kernel, column_values, precision=highest, preferred_element_type=...  117 us
    psum x3, waiting for transfers between devices, spread(): return lax.psum(block, axis)  95.1 us
    all_to_all x2, blocking collectives, shards(): lax.all_to_all(outgoing, ('row', 'col'), split_axis=0, concat_axis=0, til...  40.9 us
    dot_general x3, matrix products, shards(): jnp.einsum('enm,emr->enr', elem_mats, volume_field, precision=highest)  33 us
    all_to_all x3, waiting for transfers between devices, shards(): lax.all_to_all(leaving, ('row', 'col'), split_axis=0, concat_axis=0, tile...  29.7 us
    scatter-add x3, other arithmetic, shards(): flux_field = jnp.zeros_like(volume_flat).at[flux_take.reshape(-1)].add(la...  22.9 us
    unnamed x35, local copies, waits for them, and re-layouts  15.8 us
  transfers between devices with their start and end apart: 13, of which 12 were waited for; matrix products, arithmetic and copies ran while one was open for 23% of the time, Pallas kernels for 0%

commit v1 on v0

v1 whole, which is shorter than its diff:
```python
import jax
import jax.numpy as jnp
from jax import lax
from jax.sharding import PartitionSpec as P

ITERS = 3


boundary_step = 0.5
volume_step = 0.6
face_weight = 0.5


def passed_along(block, axis, distance):
    devices = range(lax.axis_size(axis))
    route = [(i - distance, i) for i in devices if i - distance in devices]
    return lax.ppermute(block, axis, route)


def halves(block, axis):
    high = lax.reduce_precision(block, 8, 7)
    low = block - high
    return jnp.concatenate([high.astype(jnp.bfloat16), low.astype(jnp.bfloat16)], axis=axis)


def summed(wide, columns):
    return wide[..., :columns] + wide[..., columns:]


def block_plan(owner_blocks, slot_blocks, device_self, capacity):
    mine_rows = owner_blocks == device_self
    rank_rows = jnp.cumsum(mine_rows.astype(jnp.int32), axis=1) - 1
    places = jnp.arange(capacity, dtype=jnp.int32)
    select = mine_rows[:, None, :] & (rank_rows[:, None, :] == places[None, :, None])
    index = jnp.sum(jnp.where(select, slot_blocks[:, None, :], 0), axis=2)
    valid_slot = jnp.any(select, axis=2)
    return (index, valid_slot)


def shards(
    boundary_start,
    volume_start,
    diag_part,
    incident,
    kernel,
    elem_mats,
    trace_owner,
    trace_slot,
    return_owner,
    return_slot,
    face_match,
):
    devices = lax.axis_size(("row", "col"))
    row_devices = lax.axis_size("row")
    col_devices = lax.axis_size("col")
    device_self = lax.axis_index(("row", "col"))
    row_index = lax.axis_index("row")
    col_index = lax.axis_index("col")
    total_rows = trace_slot.shape[0]
    share_rows = total_rows // devices
    capacity = max(2, 2 * share_rows // devices)
    per_panel = col_devices // row_devices
    elem_count, node_count, columns = volume_start.shape
    face_count = face_match.shape[1]
    row_panel = boundary_start.shape[0]
    positions = jnp.arange(share_rows, dtype=jnp.int32)
    trace_blocks = trace_owner[:, 0].reshape(devices, share_rows)
    trace_slots = trace_slot.reshape(devices, share_rows)
    return_blocks = return_owner[:, 0].reshape(devices, share_rows)
    return_slots = return_slot.reshape(devices, share_rows)

    route = []
    for c in range(col_devices):
        for j in range(row_devices):
            source = (c // per_panel) * col_devices + (c % per_panel) * row_devices + j
            route.append((source, j * col_devices + c))

    trace_send, trace_send_ok = block_plan(trace_blocks, trace_slots, device_self, capacity)
    own_trace = lax.dynamic_slice_in_dim(trace_blocks, row_index * col_devices, col_devices, 0)
    block_places = jnp.arange(col_devices, dtype=jnp.int32)[:, None] * share_rows + positions[None, :]
    trace_take = jax.vmap(lambda r: block_plan(own_trace, block_places, r * col_devices + col_index, capacity)[0])(
        jnp.arange(row_devices, dtype=jnp.int32)
    )
    own_return = lax.dynamic_slice_in_dim(return_blocks, col_index * row_devices, row_devices, 0)
    panel_places = jnp.arange(row_devices, dtype=jnp.int32)[:, None] * share_rows + positions[None, :]
    flux_send, flux_send_ok = jax.vmap(
        lambda d: block_plan(own_return, panel_places, row_index * col_devices + d, capacity)
    )(jnp.arange(col_devices, dtype=jnp.int32))
    flux_take, _ = block_plan(return_blocks, return_slots, device_self, capacity)
    slots = devices * capacity
    trace_send, trace_send_ok = trace_send.reshape(slots), trace_send_ok.reshape(slots, 1)
    flux_send, flux_send_ok = flux_send.reshape(slots), flux_send_ok.reshape(slots, 1)
    trace_take, flux_take = trace_take.reshape(slots), flux_take.reshape(slots)

    kernel_halves = halves(kernel, 1)
    elem_halves = halves(elem_mats, 2)
    share = lax.dynamic_slice_in_dim(boundary_start, col_index * share_rows, share_rows, 0)
    volume_field = volume_start
    for sweep_index in range(ITERS):
        moved = lax.ppermute(share, ("row", "col"), route)
        panel = lax.all_gather(moved, "row", axis=0, tiled=True)

        volume_flat = volume_field.reshape(elem_count * node_count, columns)
        outgoing = jnp.where(trace_send_ok, volume_flat[trace_send], 0.0)
        arrived = lax.all_to_all(outgoing, "row", split_axis=0, concat_axis=0, tiled=True)
        traced = jnp.zeros((row_panel, columns), jnp.float32).at[trace_take].add(arrived)

        wide = halves(panel, 1)
        image = summed(
            jnp.dot(kernel_halves, jnp.concatenate([wide, wide], 0), preferred_element_type=jnp.float32),
            columns,
        )
        residual = lax.psum_scatter(image - traced, "col", scatter_dimension=0, tiled=True)
        share = share - boundary_step * (residual + (diag_part[:, None] * share - incident))

        leaving = jnp.where(flux_send_ok, panel[flux_send], 0.0)
        landed = lax.all_to_all(leaving, "col", split_axis=0, concat_axis=0, tiled=True)
        flux_field = jnp.zeros_like(volume_flat).at[flux_take].add(landed).reshape(volume_field.shape)
        lower_faces = passed_along(volume_field[:, node_count - face_count :, :], ("row", "col"), 1)
        matched = jax.vmap(lambda face_rows, face_order: face_rows[face_order])(lower_faces, face_match)
        volume_wide = halves(volume_field, 2)
        applied = summed(
            jnp.einsum(
                "enm,emr->enr",
                elem_halves,
                jnp.concatenate([volume_wide, volume_wide], 1),
                preferred_element_type=jnp.float32,
            ),
            columns,
        )
        updated = volume_field - volume_step * (volume_field + applied - flux_field)
        volume_field = updated.at[:, :face_count, :].add(volume_step * face_weight * matched)
    boundary_final = lax.all_gather(share, "col", axis=0, tiled=True)
    return (boundary_final, volume_field)


def solution(mesh):
    placed = (
        P("row", None),
        P(("row", "col"), None, None),
        P(("row", "col")),
        P(("row", "col"), None),
        P("row", "col"),
        P(("row", "col"), None, None),
        P(),
        P(),
        P(),
        P(),
        P(("row", "col"), None),
    )
    return jax.shard_map(
        shards,
        mesh=mesh,
        in_specs=placed,
        out_specs=(P("row", None), P(("row", "col"), None, None)),
        check_vma=False,
    )
```

time: 605 us -> 563 us (0.931)
  other arithmetic: 53.7 us -> 144 us
  matrix products: 150 us -> 79.2 us
  waiting for transfers between devices: 264 us -> 194 us
  starting transfers between devices: 28.6 us -> 45 us
  blocking collectives: 40.9 us -> 31.3 us
    psum x6 -> x0, waiting for transfers between devices: 223 us -> none  [the longest x3 128 us: shards(): residual = lax.psum(partial_value, 'col')]
    reduce_scatter x0 -> x3, waiting for transfers between devices: none -> 108 us  [shards(): lax.psum_scatter(image - traced, 'col', scatter_dimension=0, tiled=True)]
    dot_general x6, matrix products: 150 us -> 79.2 us  [the longest x3 61.2 us: shards(): jnp.dot(kernel_halves, jnp.concatenate([wide, wide], 0), preferred_elemen...]
    all_gather x0 -> x4, waiting for transfers between devices: none -> 45.4 us  [the longest x3 45.4 us: shards(): panel = lax.all_gather(moved, 'row', axis=0, tiled=True)]
    convert_element_type x0 -> x8, other arithmetic: none -> 41.6 us  [halves(): high.astype(jnp.bfloat16)]
    scatter-add x3 -> x6, other arithmetic: 22.9 us -> 46.2 us  [the longest x3 23.3 us: shards(): jnp.zeros((row_panel, columns), jnp.float32).at[trace_take].add(arrived)]
    sub x3 -> x9, other arithmetic: 7.36 us -> 29.6 us  [the longest x3 13.5 us: shards(): image - traced]
    ppermute x3, starting transfers between devices: 7.03 us -> 22.2 us  [passed_along(): return lax.ppermute(block, axis, route)]
  transfers between devices with their start and end apart: 13 -> 18, of which waited for: 12 -> 9; matrix products, arithmetic and copies ran while one was open for 23% -> 31% of each run, Pallas kernels for 0% -> 0%
where the time goes in v1:
time: 563 us; the launch traced here: 553 us
  waiting for transfers between devices  194 us (34%)
  other arithmetic  144 us (26%)
  matrix products  79.2 us (14%)
  starting transfers between devices  45 us (8%)
  local copies, waits for them, and re-layouts  44.8 us (8%)
  blocking collectives  31.3 us (6%)
  between operations  15.3 us (3%)
    reduce_scatter x3, waiting for transfers between devices, shards(): lax.psum_scatter(image - traced, 'col', scatter_dimension=0, tiled=True)  108 us
    dot_general x3, matrix products, shards(): jnp.dot(kernel_halves, jnp.concatenate([wide, wide], 0), preferred_elemen...  61.2 us
    all_gather x3, waiting for transfers between devices, shards(): panel = lax.all_gather(moved, 'row', axis=0, tiled=True)  45.4 us
    convert_element_type x8, other arithmetic, halves(): high.astype(jnp.bfloat16)  41.6 us
    all_to_all x3, waiting for transfers between devices, shards(): lax.all_to_all(leaving, 'col', split_axis=0, concat_axis=0, tiled=True)  40.6 us
    all_to_all x1, blocking collectives, shards(): lax.all_to_all(outgoing, 'row', split_axis=0, concat_axis=0, tiled=True)  31.3 us
    scatter-add x3, other arithmetic, shards(): jnp.zeros((row_panel, columns), jnp.float32).at[trace_take].add(arrived)  23.3 us
    scatter-add x3, other arithmetic, shards(): jnp.zeros_like(volume_flat).at[flux_take].add(landed)  23 us
  transfers between devices with their start and end apart: 18, of which 9 were waited for; matrix products, arithmetic and copies ran while one was open for 31% of the time, Pallas kernels for 0%

profile of v1, /device:TPU:0, one launch (start us, length us, event | category | flops | bytes accessed | tf_op | source)
XLA Modules:
  0.0 553.1 jit_solution(3116891728309273738)
XLA Ops:
  11.4 5.6 %collective-permute-start.2 = (f32[8,64,128]{2,1,0:T(8,128)}, f32[8,64,128]{2,1,0:T(8,128)S(1)}, u32[]{:S(2)}, u32[]{:S(2)}) collective-permute-start(f32[8,64,128]{2,1,0:T(8,128)} %slice.156), channel_id=1, source_target_pairs={{0,1},{1,2},{2,3},{3,4},{4,5},{5,6},{6,7},{7,8},{8,9},{9,10},{10,1... | collective-permute-start | bytes 786440 | tf_op jit(solution)/shard_map/ppermute | solution.py:17
  23.9 4.5 reduce-window.36
  34.5 4.5 reduce-window.26
  39.7 24.5 %reduce-precision_convert_fusion = (bf16[4096,2048]{1,0:T(8,128)(2,1)}, bf16[4096,2048]{1,0:T(8,128)(2,1)}) fusion(f32[4096,2048]{1,0:T(8,128)} %param.21), kind=kLoop, calls=%fused_computation.16 | loop fusion | flops 33554432 | bytes 67108864 | tf_op jit(solution)/shard_map/convert_element_type | solution.py:23
  69.5 7.1 %reduce-precision_convert_fusion.1 = (bf16[8,512,512]{2,1,0:T(8,128)(2,1)S(1)}, bf16[8,512,512]{2,1,0:T(8,128)(2,1)}) fusion(f32[8,512,512]{2,1,0:T(8,128)} %param.22), kind=kLoop, calls=%fused_computation.20 | loop fusion | flops 8388608 | bytes 16777216 | tf_op jit(solution)/shard_map/convert_element_type | solution.py:23
  78.5 5.5 fusion.5
  84.0 15.2 %all-gather.5.cloned.1.call-done = f32[2048,128]{1,0:T(8,128)} async-done(((f32[512,128]{1,0:T(8,128)}), f32[2048,128]{1,0:T(8,128)}) %all-gather.5.cloned.1.call-update) | async-done | bytes 1048592 | tf_op jit(solution)/shard_map/all_gather | solution.py:101
  104.3 4.8 all-to-all-start.1
  114.0 10.4 %all-to-all-done.1 = f32[8,128,128]{2,1,0:T(8,128)S(1)} async-done(((f32[8,128,128]{2,1,0:T(8,128)}), f32[8,128,128]{2,1,0:T(8,128)S(1)}, u32[]{:S(2)}, u32[]{:S(2)}) %all-to-all-start.1) | async-done | bytes 524320 | tf_op jit(solution)/shard_map/all_to_all | solution.py:117
  124.4 7.5 %scatter_custom_fusion.1 = f32[4096,128]{1,0:T(8,128)} fusion(s32[1024]{0:T(1024)S(1)} %bitcast.77, f32[1024,128]{1,0:T(8,128)S(1)} %bitcast.67, f32[]{:T(128)} %constant.113.clone.1), kind=kCustom, calls=%fused_computation.132 | custom fusion | flops 131072 | bytes 2097156 | tf_op jit(solution)/shard_map/scatter-add | solution.py:118
  145.6 20.8 %fusion.3 = f32[4096,256]{1,0:T(8,128)} fusion(bf16[4096,2048]{1,0:T(8,128)(2,1)} %get-tuple-element.39, bf16[4096,2048]{1,0:T(8,128)(2,1)} %get-tuple-element.38, bf16[2048,128]{1,0:T(8,128)(2,1)} %get-tuple-element.53, bf16[2048,128]{1,0:T(8,128)(2,1)} %get-tuple-element.52), kind=kOutput, calls=%fused_computation.23 | convolution fusion | flops 8665432064 | bytes 38797312 | tf_op jit(solution)/shard_map/dot_general | solution.py:110
  166.3 7.6 %scatter_custom_fusion = f32[4096,128]{1,0:T(8,128)} fusion(s32[1024]{0:T(1024)S(1)} %bitcast.80, f32[1024,128]{1,0:T(8,128)S(1)} %bitcast.69, f32[]{:T(128)} %constant.113.clone.1), kind=kCustom, calls=%fused_computation.134 | custom fusion | flops 131072 | bytes 2097156 | tf_op jit(solution)/shard_map/scatter-add | solution.py:106
  174.0 4.5 fusion.46
  178.5 36.0 %reduce-scatter.4.cloned.1.call-done = f32[512,128]{1,0:T(8,128)} async-done(((f32[4096,128]{1,0:T(8,128)}), f32[512,128]{1,0:T(8,128)}) %reduce-scatter.4.cloned.1.call-update) | async-done | bytes 262160 | tf_op jit(solution)/shard_map/reduce_scatter | solution.py:113
  217.2 31.3 %all_to_all.54 = f32[4,256,128]{2,1,0:T(8,128)} all-to-all(f32[4,256,128]{2,1,0:T(8,128)S(1)} %get-tuple-element.56), channel_id=1, replica_groups=mesh['row'=4,'col'=8] {'row'}, dimensions={0} | all-to-all | bytes 1048576 | tf_op jit(solution)/shard_map/all_to_all | solution.py:105
  248.5 8.0 %scatter_custom_fusion.2 = f32[4096,128]{1,0:T(8,128)} fusion(s32[1024]{0:T(1024)S(1)} %bitcast.81, f32[1024,128]{1,0:T(8,128)} %bitcast.71, f32[]{:T(128)} %constant.113.clone.1), kind=kCustom, calls=%fused_computation.130 | custom fusion | flops 131072 | bytes 2097664 | tf_op jit(solution)/shard_map/scatter-add | solution.py:106
  256.5 5.7 %all-gather.7.cloned.1.call-done = f32[2048,128]{1,0:T(8,128)} async-done(((f32[512,128]{1,0:T(8,128)}), f32[2048,128]{1,0:T(8,128)}) %all-gather.7.cloned.1.call-update) | async-done | bytes 1048592 | tf_op jit(solution)/shard_map/all_gather | solution.py:101
  264.4 20.2 %fusion.2 = f32[4096,256]{1,0:T(8,128)} fusion(bf16[4096,2048]{1,0:T(8,128)(2,1)} %get-tuple-element.39, bf16[4096,2048]{1,0:T(8,128)(2,1)} %get-tuple-element.38, bf16[2048,128]{1,0:T(8,128)(2,1)} %get-tuple-element.51, bf16[2048,128]{1,0:T(8,128)(2,1)S(1)} %get-tuple-element.50), kind=kOutput, calls=%fused_computation.22 | convolution fusion | flops 8665432064 | bytes 38797312 | tf_op jit(solution)/shard_map/dot_general | solution.py:110
  289.2 36.0 %reduce-scatter.6.cloned.1.call-done = f32[512,128]{1,0:T(8,128)} async-done(((f32[4096,128]{1,0:T(8,128)}), f32[512,128]{1,0:T(8,128)}) %reduce-scatter.6.cloned.1.call-update) | async-done | bytes 262160 | tf_op jit(solution)/shard_map/reduce_scatter | solution.py:113
  329.3 15.3 %collective-permute-start.4 = (f32[8,64,128]{2,1,0:T(8,128)}, f32[8,64,128]{2,1,0:T(8,128)S(1)}, u32[]{:S(2)}, u32[]{:S(2)}) collective-permute-start(f32[8,64,128]{2,1,0:T(8,128)} %slice.203), channel_id=1, source_target_pairs={{0,1},{1,2},{2,3},{3,4},{4,5},{5,6},{6,7},{7,8},{8,9},{9,10},{10,1... | collective-permute-start | bytes 786440 | tf_op jit(solution)/shard_map/ppermute | solution.py:17
  349.2 24.5 %all-gather.9.cloned.1.call-done = f32[2048,128]{1,0:T(8,128)} async-done(((f32[512,128]{1,0:T(8,128)}), f32[2048,128]{1,0:T(8,128)}) %all-gather.9.cloned.1.call-update) | async-done | bytes 1048592 | tf_op jit(solution)/shard_map/all_gather | solution.py:101
  378.9 4.6 all-to-all-start.3
  383.6 6.2 %fusion.13 = f32[8,512,256]{2,1,0:T(8,128)} fusion(bf16[8,512,128]{2,1,0:T(8,128)(2,1)S(1)} %copy-done.12, bf16[8,512,128]{2,1,0:T(8,128)(2,1)S(1)} %copy-done.11, bf16[8,512,512]{2,1,0:T(8,128)(2,1)} %get-tuple-element.41, bf16[8,512,512]{2,1,0:T(8,128)(2,1)} %copy-done.6), kind=kOutput, calls=%fused_computation.34 | convolution fusion | flops 2181038080 | bytes 14680064 | tf_op jit(solution)/shard_map/enm,emr->enr/dot_general | solution.py:123
  394.4 4.6 all-to-all-done.3
  399.0 8.1 %scatter_custom_fusion.3 = f32[4096,128]{1,0:T(8,128)} fusion(s32[1024]{0:T(1024)S(1)} %bitcast.78, f32[1024,128]{1,0:T(8,128)} %bitcast.22, f32[]{:T(128)} %constant.113.clone.1), kind=kCustom, calls=%fused_computation.128 | custom fusion | flops 131072 | bytes 2097664 | tf_op jit(solution)/shard_map/scatter-add | solution.py:118
  418.4 20.3 %fusion.1 = f32[4096,256]{1,0:T(8,128)} fusion(bf16[4096,2048]{1,0:T(8,128)(2,1)} %get-tuple-element.39, bf16[4096,2048]{1,0:T(8,128)(2,1)} %get-tuple-element.38, bf16[2048,128]{1,0:T(8,128)(2,1)} %get-tuple-element.49, bf16[2048,128]{1,0:T(8,128)(2,1)S(1)} %get-tuple-element.48), kind=kOutput, calls=%fused_computation.21 | convolution fusion | flops 8665432064 | bytes 38797312 | tf_op jit(solution)/shard_map/dot_general | solution.py:110
  438.7 7.6 %scatter_custom_fusion.4 = f32[4096,128]{1,0:T(8,128)} fusion(s32[1024]{0:T(1024)S(1)} %bitcast.82, f32[1024,128]{1,0:T(8,128)S(1)} %bitcast.68, f32[]{:T(128)} %constant.113.clone.1), kind=kCustom, calls=%fused_computation.126 | custom fusion | flops 131072 | bytes 2097156 | tf_op jit(solution)/shard_map/scatter-add | solution.py:106
  446.3 4.5 fusion.40
  450.9 35.9 %reduce-scatter.8.cloned.1.call-done = f32[512,128]{1,0:T(8,128)} async-done(((f32[4096,128]{1,0:T(8,128)}), f32[512,128]{1,0:T(8,128)}) %reduce-scatter.8.cloned.1.call-update) | async-done | bytes 262160 | tf_op jit(solution)/shard_map/reduce_scatter | solution.py:113
  492.1 25.6 %all-to-all-done.5 = f32[8,128,128]{2,1,0:T(8,128)S(1)} async-done(((f32[8,128,128]{2,1,0:T(8,128)}), f32[8,128,128]{2,1,0:T(8,128)S(1)}, u32[]{:S(2)}, u32[]{:S(2)}) %all-to-all-start.5) | async-done | bytes 524320 | tf_op jit(solution)/shard_map/all_to_all | solution.py:117
  517.8 7.5 %scatter_custom_fusion.5 = f32[4096,128]{1,0:T(8,128)} fusion(s32[1024]{0:T(1024)S(1)} %bitcast.79, f32[1024,128]{1,0:T(8,128)S(1)} %bitcast.70, f32[]{:T(128)} %constant.113.clone.1), kind=kCustom, calls=%fused_computation.124 | custom fusion | flops 131072 | bytes 2097156 | tf_op jit(solution)/shard_map/scatter-add | solution.py:118
  527.0 6.3 %fusion.21 = f32[8,512,256]{2,1,0:T(8,128)} fusion(bf16[8,512,128]{2,1,0:T(8,128)(2,1)S(1)} %get-tuple-element.43, bf16[8,512,128]{2,1,0:T(8,128)(2,1)S(1)} %get-tuple-element.42, bf16[8,512,512]{2,1,0:T(8,128)(2,1)} %get-tuple-element.41, bf16[8,512,512]{2,1,0:T(8,128)(2,1)} %copy-done.6), kind=kOutput, calls=%fused_computation.42 | convolution fusion | flops 2181038080 | bytes 14680064 | tf_op jit(solution)/shard_map/enm,emr->enr/dot_general | solution.py:123
  (182 shorter events, 107.2 us)
Async XLA Ops:
  7.2 16.4 %copy-start.19 = (s32[16384,1]{0,1:T(1,128)S(1)}, s32[16384,1]{0,1:T(1,128)}, u32[]{:S(2)}) copy-start(s32[16384,1]{0,1:T(1,128)} %param.25) | copy-start | bytes 196612
  7.2 24.8 %copy-start.20 = (s32[16384]{0:T(1024)S(1)}, s32[16384]{0:T(1024)}, u32[]{:S(2)}) copy-start(s32[16384]{0:T(1024)} %param.26) | copy-start | bytes 196612
  7.2 24.8 %copy-start.23 = (s32[8,64]{1,0:T(8,128)S(1)}, s32[8,64]{1,0:T(8,128)}, u32[]{:S(2)}) copy-start(s32[8,64]{1,0:T(8,128)} %param.27) | copy-start | bytes 6148
  7.2 92.0 %all-gather.5.cloned.1.call-start = ((), (), s32[]{:S(2)}) async-start(), calls=%async_computation.9 | async-start | bytes 1310720 | tf_op jit(solution)/shard_map/all_gather | solution.py:101
  7.3 26.3 %copy-start.21 = (s32[16384]{0:T(1024)S(1)}, s32[16384]{0:T(1024)}, u32[]{:S(2)}) copy-start(s32[16384]{0:T(1024)} %param.24) | copy-start | bytes 196612
  8.3 61.1 %collective-permute-start = (f32[512,128]{1,0:T(8,128)S(1)}, f32[512,128]{1,0:T(8,128)}, u32[]{:S(2)}, u32[]{:S(2)}) collective-permute-start(f32[512,128]{1,0:T(8,128)S(1)} %constant_dynamic-slice_fusion.2), channel_id=1, source_target_pairs={{0,0},{1,8},{2,16},{3,24},{4,1},{5,9},{6,17},{7,25},{8,2},{9,10},{... | collective-permute-start | bytes 786440 | tf_op jit(solution)/shard_map/ppermute | solution.py:100
  11.4 97.8 %collective-permute-start.2 = (f32[8,64,128]{2,1,0:T(8,128)}, f32[8,64,128]{2,1,0:T(8,128)S(1)}, u32[]{:S(2)}, u32[]{:S(2)}) collective-permute-start(f32[8,64,128]{2,1,0:T(8,128)} %slice.156), channel_id=1, source_target_pairs={{0,1},{1,2},{2,3},{3,4},{4,5},{5,6},{6,7},{7,8},{8,9},{9,10},{10,1... | collective-permute-start | bytes 786440 | tf_op jit(solution)/shard_map/ppermute | solution.py:17
  39.7 26.9 %copy-start.1 = (f32[8,512,128]{2,1,0:T(8,128)S(1)}, f32[8,512,128]{2,1,0:T(8,128)}, u32[]{:S(2)}) copy-start(f32[8,512,128]{2,1,0:T(8,128)} %param.18) | copy-start | bytes 6291460
  104.3 20.1 %all-to-all-start.1 = ((f32[8,128,128]{2,1,0:T(8,128)}), f32[8,128,128]{2,1,0:T(8,128)S(1)}, u32[]{:S(2)}, u32[]{:S(2)}) async-start(f32[8,128,128]{2,1,0:T(8,128)} %broadcast_select_fusion.2), calls=%async_computation.2 | async-start | bytes 1048576 | tf_op jit(solution)/shard_map/all_to_all | solution.py:117
  135.9 208.7 %copy-start = (f32[8,512,128]{2,1,0:T(8,128)}, f32[8,512,128]{2,1,0:T(8,128)S(1)}, u32[]{:S(2)}) copy-start(f32[8,512,128]{2,1,0:T(8,128)S(1)} %fusion.91) | copy-start | bytes 6291460
  142.0 24.3 %all-to-all-start = ((f32[4,256,128]{2,1,0:T(8,128)}), f32[4,256,128]{2,1,0:T(8,128)S(1)}, u32[]{:S(2)}, u32[]{:S(2)}) async-start(f32[4,256,128]{2,1,0:T(8,128)} %get-tuple-element.57), calls=%async_computation | async-start | bytes 1048576 | tf_op jit(solution)/shard_map/all_to_all | solution.py:105
  145.5 69.0 %reduce-scatter.4.cloned.1.call-start = ((), (), s32[]{:S(2)}) async-start(), calls=%async_computation.10 | async-start | bytes 2359296 | tf_op jit(solution)/shard_map/reduce_scatter | solution.py:113
  173.9 40.6 %copy-start.7 = (f32[512,128]{1,0:T(8,128)S(1)}, f32[512,128]{1,0:T(8,128)}, u32[]{:S(2)}) copy-start(f32[512,128]{1,0:T(8,128)} %param.20) | copy-start | bytes 786436
  173.9 40.6 %copy-start.22 = (f32[512]{0:T(512)S(1)}, f32[512]{0:T(512)}, u32[]{:S(2)}) copy-start(f32[512]{0:T(512)} %param.19) | copy-start | bytes 6148
  178.5 83.7 %all-gather.7.cloned.1.call-start = ((), (), s32[]{:S(2)}) async-start(), calls=%async_computation.11 | async-start | bytes 1310720 | tf_op jit(solution)/shard_map/all_gather | solution.py:101
  215.7 69.0 %copy-start.15 = (f32[512,128]{1,0:T(8,128)}, f32[512,128]{1,0:T(8,128)S(1)}, u32[]{:S(2)}) copy-start(f32[512,128]{1,0:T(8,128)S(1)} %multiply_subtract_fusion.2) | copy-start | bytes 786436
  215.7 0.7 collective-permute-start.1
  217.1 108.1 %reduce-scatter.6.cloned.1.call-start = ((), (), s32[]{:S(2)}) async-start(), calls=%async_computation.12 | async-start | bytes 2359296 | tf_op jit(solution)/shard_map/reduce_scatter | solution.py:113
  289.1 57.2 %copy-start.2 = (f32[2048,128]{1,0:T(8,128)S(1)}, f32[2048,128]{1,0:T(8,128)}, u32[]{:S(2)}) copy-start(f32[2048,128]{1,0:T(8,128)} %all-gather.7.cloned.1.call-done) | copy-start | bytes 3145732
  289.2 84.5 %all-gather.9.cloned.1.call-start = ((), (), s32[]{:S(2)}) async-start(), calls=%async_computation.13 | async-start | bytes 1310720 | tf_op jit(solution)/shard_map/all_gather | solution.py:101
  327.1 0.7 collective-permute-start.3
  329.3 60.5 %collective-permute-start.4 = (f32[8,64,128]{2,1,0:T(8,128)}, f32[8,64,128]{2,1,0:T(8,128)S(1)}, u32[]{:S(2)}, u32[]{:S(2)}) collective-permute-start(f32[8,64,128]{2,1,0:T(8,128)} %slice.203), channel_id=1, source_target_pairs={{0,1},{1,2},{2,3},{3,4},{4,5},{5,6},{6,7},{7,8},{8,9},{9,10},{10,1... | collective-permute-start | bytes 786440 | tf_op jit(solution)/shard_map/ppermute | solution.py:17
  349.2 34.4 %copy-start.11 = (bf16[8,512,128]{2,1,0:T(8,128)(2,1)S(1)}, bf16[8,512,128]{2,1,0:T(8,128)(2,1)}, u32[]{:S(2)}) copy-start(bf16[8,512,128]{2,1,0:T(8,128)(2,1)} %get-tuple-element.44) | copy-start | bytes 3145732
  349.2 34.4 %copy-start.12 = (bf16[8,512,128]{2,1,0:T(8,128)(2,1)S(1)}, bf16[8,512,128]{2,1,0:T(8,128)(2,1)}, u32[]{:S(2)}) copy-start(bf16[8,512,128]{2,1,0:T(8,128)(2,1)} %get-tuple-element.45) | copy-start | bytes 3145732
  378.9 20.0 %all-to-all-start.3 = ((f32[8,128,128]{2,1,0:T(8,128)}), f32[8,128,128]{2,1,0:T(8,128)}, u32[]{:S(2)}, u32[]{:S(2)}) async-start(f32[8,128,128]{2,1,0:T(8,128)} %get-tuple-element.55), calls=%async_computation.5 | async-start | bytes 1048576 | tf_op jit(solution)/shard_map/all_to_all | solution.py:117
  414.9 23.8 %all-to-all-start.4 = ((f32[4,256,128]{2,1,0:T(8,128)}), f32[4,256,128]{2,1,0:T(8,128)S(1)}, u32[]{:S(2)}, u32[]{:S(2)}) async-start(f32[4,256,128]{2,1,0:T(8,128)} %broadcast_select_fusion.3), calls=%async_computation.6 | async-start | bytes 1048576 | tf_op jit(solution)/shard_map/all_to_all | solution.py:105
  418.4 68.4 %reduce-scatter.8.cloned.1.call-start = ((), (), s32[]{:S(2)}) async-start(), calls=%async_computation.14 | async-start | bytes 2359296 | tf_op jit(solution)/shard_map/reduce_scatter | solution.py:113
  446.3 40.5 %copy-start.8 = (f32[512,128]{1,0:T(8,128)S(1)}, f32[512,128]{1,0:T(8,128)}, u32[]{:S(2)}) copy-start(f32[512,128]{1,0:T(8,128)} %param.20) | copy-start | bytes 786436
  446.3 40.5 %copy-start.14 = (f32[512,128]{1,0:T(8,128)S(1)}, f32[512,128]{1,0:T(8,128)}, u32[]{:S(2)}) copy-start(f32[512,128]{1,0:T(8,128)} %copy-done.13) | copy-start | bytes 786436
  450.8 91.9 %all-gather.11.cloned.1.call-start = ((), (), s32[]{:S(2)}) async-start(), calls=%async_computation.15 | async-start | bytes 2359296 | tf_op jit(solution)/shard_map/all_gather | solution.py:133
  488.6 29.2 %all-to-all-start.5 = ((f32[8,128,128]{2,1,0:T(8,128)}), f32[8,128,128]{2,1,0:T(8,128)S(1)}, u32[]{:S(2)}, u32[]{:S(2)}) async-start(f32[8,128,128]{2,1,0:T(8,128)} %get-tuple-element.54), calls=%async_computation.8 | async-start | bytes 1048576 | tf_op jit(solution)/shard_map/all_to_all | solution.py:117
  525.2 12.2 %collective-permute-start.5 = (f32[8,64,128]{2,1,0:T(8,128)S(1)}, f32[8,64,128]{2,1,0:T(8,128)S(1)}, u32[]{:S(2)}, u32[]{:S(2)}) collective-permute-start(f32[8,64,128]{2,1,0:T(8,128)S(1)} %slice.207), channel_id=1, source_target_pairs={{0,1},{1,2},{2,3},{3,4},{4,5},{5,6},{6,7},{7,8},{8,9},{9,10},{10,1... | collective-permute-start | bytes 786440 | tf_op jit(solution)/shard_map/ppermute | solution.py:17
  (10 other events, 67.6 us)
Sparse Core Ops, SparseCore 0:
  69.5 29.6 all-gather.4
  178.6 35.8 reduce-scatter.3
  217.2 44.9 all-gather.6
  289.3 35.9 reduce-scatter.5
  328.6 45.0 all-gather.8
  451.0 35.7 reduce-scatter.7
  488.9 36.7 all-gather.10

commit v2 on v1

--- a/solution.py
+++ b/solution.py
@@ -1,6 +1,10 @@
+import functools
+
 import jax
 import jax.numpy as jnp
 from jax import lax
+from jax.experimental import pallas as pl
+from jax.experimental.pallas import tpu as pltpu
 from jax.sharding import PartitionSpec as P
 
 ITERS = 3
@@ -15,6 +19,194 @@
     devices = range(lax.axis_size(axis))
     route = [(i - distance, i) for i in devices if i - distance in devices]
     return lax.ppermute(block, axis, route)
+
+
+def exchange_kernel(reduces, finishes, *refs):
+    rows_n, cols_n = lax.axis_size("row"), lax.axis_size("col")
+    pairs = cols_n // 2
+    per_panel = cols_n // rows_n
+    r, c = lax.axis_index("row"), lax.axis_index("col")
+    z, h = c // 2, c % 2
+    partner = z * 2 + (1 - h)
+    target_row, target_col = c % rows_n, r * per_panel + c // rows_n
+    source_row, source_col = c // per_panel, (c % per_panel) * rows_n + r
+    stays = (target_row == r) & (target_col == c)
+
+    if reduces:
+        partial, middle, refs = refs[0], refs[1], refs[2:]
+    else:
+        middle, refs = refs[0], refs[1:]
+    if finishes:
+        out, refs = refs[0], refs[1:]
+    else:
+        share, out, refs = refs[0], refs[1], refs[2:]
+    if reduces:
+        from_pair, summed_pair, from_line, refs = refs[0], refs[1], refs[2], refs[3:]
+        pair_send, pair_recv, line_send, line_recv, refs = refs[0], refs[1], refs[2], refs[3], refs[4:]
+    if finishes:
+        out_send, out_recv, back_send, back_recv = refs
+    else:
+        move_send, move_recv, row_send, row_recv = refs
+
+    barrier = pltpu.get_barrier_semaphore()
+
+    def greet(row, col):
+        pl.semaphore_signal(barrier, inc=1, device_id=(row, col), device_id_type=pl.DeviceIdType.MESH)
+
+    greeted = 0
+    if reduces:
+        greet(r, partner)
+        for step in range(1, pairs):
+            greet(r, ((z + step) % pairs) * 2 + h)
+        greeted += pairs
+    if not finishes:
+        for step in range(1, rows_n):
+            greet((r + step) % rows_n, c)
+        greeted += rows_n - 1
+
+        @pl.when(jnp.logical_not(stays))
+        def _():
+            greet(source_row, source_col)
+
+        greeted += jnp.where(stays, 0, 1)
+
+    pl.semaphore_wait(barrier, greeted)
+
+    def remote(src, dst, send, recv, row, col):
+        return pltpu.make_async_remote_copy(
+            src_ref=src,
+            dst_ref=dst,
+            send_sem=send,
+            recv_sem=recv,
+            device_id=(row, col),
+            device_id_type=pl.DeviceIdType.MESH,
+        )
+
+    if reduces:
+        pair_copies = []
+        for step in range(1, pairs + 1):
+            other = (z + step) % pairs
+            copy = remote(
+                partial.at[other * 2 + (1 - h)], from_pair.at[step - 1],
+                pair_send.at[step - 1], pair_recv.at[step - 1], r, partner,
+            )
+            copy.start()
+            pair_copies.append(copy)
+        line_copies = []
+        for step in range(1, pairs):
+            other = (z + step) % pairs
+            pair_copies[step - 1].wait_recv()
+            summed_pair[step - 1] = from_pair[step - 1] + partial[other * 2 + h]
+            copy = remote(
+                summed_pair.at[step - 1], from_line.at[step - 1],
+                line_send.at[step - 1], line_recv.at[step - 1], r, other * 2 + h,
+            )
+            copy.start()
+            line_copies.append(copy)
+        pair_copies[pairs - 1].wait_recv()
+        total = from_pair[pairs - 1] + partial[z * 2 + h]
+        summed_pair[pairs - 1] = total
+        for step in range(1, pairs):
+            line_copies[step - 1].wait_recv()
+            summed_pair[pairs - 1] += from_line[step - 1]
+        fresh = middle[...] - boundary_step * summed_pair[pairs - 1]
+        if finishes:
+            out[c] = fresh
+        else:
+            share[...] = fresh
+    else:
+        share[...] = middle[...]
+
+    if finishes:
+        sent = []
+        for step in range(1, pairs):
+            copy = remote(
+                out.at[c], out.at[c], out_send.at[step - 1], out_recv.at[step - 1],
+                r, ((z + step) % pairs) * 2 + h,
+            )
+            copy.start()
+            sent.append(copy)
+        back = [remote(out.at[c], out.at[c], back_send.at[0], back_recv.at[0], r, partner)]
+        back[0].start()
+        for step in range(1, pairs):
+            origin = ((z - step + pairs) % pairs) * 2 + h
+            sent[step - 1].wait_recv()
+            copy = remote(
+                out.at[origin], out.at[origin], back_send.at[step], back_recv.at[step], r, partner
+            )
+            copy.start()
+            back.append(copy)
+        for copy in back:
+            copy.wait_recv()
+        for copy in sent + back:
+            copy.wait_send()
+    else:
+        @pl.when(stays)
+        def _():
+            out[r] = share[...]
+
+        move = remote(share, out.at[target_row], move_send, move_recv, target_row, target_col)
+
+        @pl.when(jnp.logical_not(stays))
+        def _():
+            move.start()
+            move.wait_recv()
+
+        sent = []
+        for step in range(1, rows_n):
+            copy = remote(
+                out.at[r], out.at[r], row_send.at[step - 1], row_recv.at[step - 1],
+                (r + step) % rows_n, c,
+            )
+            copy.start()
+            sent.append(copy)
+        for copy in sent:
+            copy.wait_recv()
+        for copy in sent:
+            copy.wait_send()
+
+        @pl.when(jnp.logical_not(stays))
+        def _():
+            move.wait_send()
+
+    if reduces:
+        for copy in pair_copies + line_copies:
+            copy.wait_send()
+
+
+def exchange(reduces, finishes, *operands):
+    rows_n, cols_n = lax.axis_size("row"), lax.axis_size("col")
+    pairs = cols_n // 2
+    rows, columns = operands[-1].shape
+    block = (rows, columns)
+    in_vmem = pl.BlockSpec(memory_space=pltpu.VMEM)
+    if finishes:
+        shapes = [jax.ShapeDtypeStruct((cols_n,) + block, jnp.float32)]
+    else:
+        shapes = [
+            jax.ShapeDtypeStruct(block, jnp.float32),
+            jax.ShapeDtypeStruct((rows_n,) + block, jnp.float32),
+        ]
+    scratch = []
+    if reduces:
+        scratch += [pltpu.VMEM((pairs,) + block, jnp.float32), pltpu.VMEM((pairs,) + block, jnp.float32)]
+        scratch += [pltpu.VMEM((pairs - 1,) + block, jnp.float32)]
+        scratch += [pltpu.SemaphoreType.DMA((pairs,))] * 2 + [pltpu.SemaphoreType.DMA((pairs - 1,))] * 2
+    if finishes:
+        scratch += [pltpu.SemaphoreType.DMA((pairs - 1,))] * 2 + [pltpu.SemaphoreType.DMA((pairs,))] * 2
+    else:
+        scratch += [pltpu.SemaphoreType.DMA] * 2 + [pltpu.SemaphoreType.DMA((rows_n - 1,))] * 2
+    return pl.pallas_call(
+        functools.partial(exchange_kernel, reduces, finishes),
+        out_shape=shapes,
+        in_specs=[in_vmem] * len(operands),
+        out_specs=[in_vmem] * len(shapes),
+        scratch_shapes=scratch,
+        compiler_params=pltpu.CompilerParams(
+            collective_id=int(reduces) + int(finishes), has_side_effects=True, vmem_limit_bytes=24 << 20
+        ),
+        cost_estimate=pl.CostEstimate(flops=1000, bytes_accessed=150_000_000, transcendentals=0),
+    )(*operands)
 
 
 def halves(block, axis):
@@ -69,12 +261,6 @@
     return_blocks = return_owner[:, 0].reshape(devices, share_rows)
     return_slots = return_slot.reshape(devices, share_rows)
 
-    route = []
-    for c in range(col_devices):
-        for j in range(row_devices):
-            source = (c // per_panel) * col_devices + (c % per_panel) * row_devices + j
-            route.append((source, j * col_devices + c))
-
     trace_send, trace_send_ok = block_plan(trace_blocks, trace_slots, device_self, capacity)
     own_trace = lax.dynamic_slice_in_dim(trace_blocks, row_index * col_devices, col_devices, 0)
     block_places = jnp.arange(col_devices, dtype=jnp.int32)[:, None] * share_rows + positions[None, :]
@@ -95,10 +281,10 @@
     kernel_halves = halves(kernel, 1)
     elem_halves = halves(elem_mats, 2)
     share = lax.dynamic_slice_in_dim(boundary_start, col_index * share_rows, share_rows, 0)
+    share, panel = exchange(False, False, share)
     volume_field = volume_start
     for sweep_index in range(ITERS):
-        moved = lax.ppermute(share, ("row", "col"), route)
-        panel = lax.all_gather(moved, "row", axis=0, tiled=True)
+        panel = panel.reshape(row_devices * share_rows, columns)
 
         volume_flat = volume_field.reshape(elem_count * node_count, columns)
         outgoing = jnp.where(trace_send_ok, volume_flat[trace_send], 0.0)
@@ -110,9 +296,8 @@
             jnp.dot(kernel_halves, jnp.concatenate([wide, wide], 0), preferred_element_type=jnp.float32),
             columns,
         )
-        residual = lax.psum_scatter(image - traced, "col", scatter_dimension=0, tiled=True)
-        share = share - boundary_step * (residual + (diag_part[:, None] * share - incident))
-
+        partial_value = (image - traced).reshape(col_devices, share_rows, columns)
+        middle = share - boundary_step * (diag_part[:, None] * share - incident)
         leaving = jnp.where(flux_send_ok, panel[flux_send], 0.0)
         landed = lax.all_to_all(leaving, "col", split_axis=0, concat_axis=0, tiled=True)
         flux_field = jnp.zeros_like(volume_flat).at[flux_take].add(landed).reshape(volume_field.shape)
@@ -130,8 +315,11 @@
         )
         updated = volume_field - volume_step * (volume_field + applied - flux_field)
         volume_field = updated.at[:, :face_count, :].add(volume_step * face_weight * matched)
-    boundary_final = lax.all_gather(share, "col", axis=0, tiled=True)
-    return (boundary_final, volume_field)
+        if sweep_index < ITERS - 1:
+            share, panel = exchange(True, False, partial_value, middle)
+        else:
+            (boundary_final,) = exchange(True, True, partial_value, middle)
+    return (boundary_final.reshape(row_panel, columns), volume_field)
 
 
 def solution(mesh):

time: 563 us -> 491 us (0.87)
  Pallas kernels: 0 us -> 192 us
  waiting for transfers between devices: 194 us -> 2.06 us
  blocking collectives: 31.3 us -> 0 us
  starting transfers between devices: 45 us -> 31.1 us
  between operations: 15.3 us -> 1.53 us
  other arithmetic: 144 us -> 136 us
  local copies, waits for them, and re-layouts: 44.8 us -> 37.5 us
    pallas_call x0 -> x4, Pallas kernels: none -> 192 us  [exchange(): pl.pallas_call(functools.partial(exchange_kernel, reduces, finishes), out...]
    reduce_scatter x3 -> x0, waiting for transfers between devices: 108 us -> none  [shards(): lax.psum_scatter(image - traced, 'col', scatter_dimension=0, tiled=True)]
    all_gather x4 -> x0, waiting for transfers between devices: 45.4 us -> none  [the longest x3 45.4 us: shards(): panel = lax.all_gather(moved, 'row', axis=0, tiled=True)]
    all_to_all x3, waiting for transfers between devices: 40.6 us -> 2.05 us  [shards(): lax.all_to_all(leaving, 'col', split_axis=0, concat_axis=0, tiled=True)]
    all_to_all x1 -> x0, blocking collectives: 31.3 us -> none  [shards(): lax.all_to_all(outgoing, 'row', split_axis=0, concat_axis=0, tiled=True)]
    ppermute x3, starting transfers between devices: 22.2 us -> 7.51 us  [passed_along(): return lax.ppermute(block, axis, route)]
    sub x6, other arithmetic: 17.7 us -> 9.24 us  [the longest x3 8.85 us: shards(): partial_value = (image - traced).reshape(col_devices, share_rows, columns)]
    unnamed x50 -> x32, local copies, waits for them, and re-layouts: 7.75 us -> 2 us
  transfers between devices with their start and end apart: 18 -> 9, of which waited for: 9 -> 1; matrix products, arithmetic and copies ran while one was open for 31% -> 35% of each run, Pallas kernels for 0% -> 12%
where the time goes in v2:
time: 491 us; the launch traced here: 485 us
  Pallas kernels  192 us (39%)
  other arithmetic  136 us (28%)
  matrix products  84.6 us (17%)
  local copies, waits for them, and re-layouts  37.5 us (8%)
  starting transfers between devices  31.1 us (6%)
    pallas_call x4, Pallas kernels, exchange(): pl.pallas_call(functools.partial(exchange_kernel, reduces, finishes), out...  192 us
    dot_general x3, matrix products, shards(): jnp.dot(kernel_halves, jnp.concatenate([wide, wide], 0), preferred_elemen...  61.3 us
    convert_element_type x8, other arithmetic, halves(): high.astype(jnp.bfloat16)  43.7 us
    dot_general x3, matrix products, shards(): jnp.einsum('enm,emr->enr', elem_halves, jnp.concatenate([volume_wide, vol...  23.3 us
    scatter-add x3, other arithmetic, shards(): jnp.zeros_like(volume_flat).at[flux_take].add(landed)  22.6 us
    scatter-add x3, other arithmetic, shards(): jnp.zeros((row_panel, columns), jnp.float32).at[trace_take].add(arrived)  21.9 us
    all_to_all x3, starting transfers between devices, shards(): lax.all_to_all(leaving, 'col', split_axis=0, concat_axis=0, tiled=True)  12 us
    sub x3, other arithmetic, shards(): updated = volume_field - volume_step * (volume_field + applied - flux_field)  11.9 us
  transfers between devices with their start and end apart: 9, of which 1 were waited for; matrix products, arithmetic and copies ran while one was open for 35% of the time, Pallas kernels for 12%

profile of v2, /device:TPU:0, one launch (start us, length us, event | category | flops | bytes accessed | tf_op | source)
XLA Modules:
  0.0 484.7 jit_solution(5858435379311262937)
XLA Ops:
  3.1 4.5 reduce-window.36
  9.8 32.3 %shard_map.122 = (f32[512,128]{1,0:T(8,128)S(1)}, f32[4,512,128]{2,1,0:T(8,128)S(1)}) custom-call(f32[512,128]{1,0:T(8,128)S(1)} %constant_dynamic-slice_fusion.2.refs_0_), custom_call_target="tpu_custom_call" | custom-call | flops 1000 | bytes 150000000 | tf_op jit(solution)/shard_map/pallas_call | solution.py:199
  46.0 3.5 all-to-all-start.1
  62.1 8.2 %reduce-precision_convert_fusion.1 = (bf16[8,512,512]{2,1,0:T(8,128)(2,1)}, bf16[8,512,512]{2,1,0:T(8,128)(2,1)}) fusion(f32[8,512,512]{2,1,0:T(8,128)} %param.22), kind=kLoop, calls=%fused_computation.20 | loop fusion | flops 8388608 | bytes 16777216 | tf_op jit(solution)/shard_map/convert_element_type | solution.py:215
  72.7 4.5 reduce-window.26
  77.9 25.4 %reduce-precision_convert_fusion = (bf16[4096,2048]{1,0:T(8,128)(2,1)}, bf16[4096,2048]{1,0:T(8,128)(2,1)}) fusion(f32[4096,2048]{1,0:T(8,128)} %param.21), kind=kLoop, calls=%fused_computation.16 | loop fusion | flops 33554432 | bytes 67108864 | tf_op jit(solution)/shard_map/convert_element_type | solution.py:215
  103.3 5.5 %fusion.5 = f32[8,512,256]{2,1,0:T(8,128)} fusion(bf16[8,512,128]{2,1,0:T(8,128)(2,1)S(1)} %copy-done.7, bf16[8,512,128]{2,1,0:T(8,128)(2,1)S(1)} %get-tuple-element.58, bf16[8,512,512]{2,1,0:T(8,128)(2,1)} %get-tuple-element.53, bf16[8,512,512]{2,1,0:T(8,128)(2,1)S(1)} %copy-done.4), kind=kOutput, calls=%fused_computation.26 | convolution fusion | flops 2181038080 | bytes 14680064 | tf_op jit(solution)/shard_map/enm,emr->enr/dot_general | solution.py:308
  108.8 20.4 %fusion.3 = f32[4096,256]{1,0:T(8,128)} fusion(bf16[4096,2048]{1,0:T(8,128)(2,1)} %get-tuple-element.51, bf16[4096,2048]{1,0:T(8,128)(2,1)} %get-tuple-element.50, bf16[2048,128]{1,0:T(8,128)(2,1)} %get-tuple-element.65, bf16[2048,128]{1,0:T(8,128)(2,1)S(1)} %copy-done.8), kind=kOutput, calls=%fused_computation.23 | convolution fusion | flops 8665432064 | bytes 38797312 | tf_op jit(solution)/shard_map/dot_general | solution.py:296
  130.7 4.4 gather_fusion
  135.3 3.7 gather_fusion.6
  139.0 7.6 %scatter_custom_fusion.1 = f32[4096,128]{1,0:T(8,128)} fusion(s32[1024]{0:T(1024)S(1)} %bitcast.98, f32[1024,128]{1,0:T(8,128)S(1)} %bitcast.87, f32[]{:T(128)} %constant.113.clone.1), kind=kCustom, calls=%fused_computation.132 | custom fusion | flops 131072 | bytes 2097156 | tf_op jit(solution)/shard_map/scatter-add | solution.py:303
  146.6 3.9 fusion.44
  152.7 4.4 gather_fusion.2
  158.3 4.3 all-to-all-start
  165.8 8.8 %fusion.13 = f32[8,512,256]{2,1,0:T(8,128)} fusion(bf16[8,512,128]{2,1,0:T(8,128)(2,1)} %get-tuple-element.57, bf16[8,512,128]{2,1,0:T(8,128)(2,1)} %get-tuple-element.56, bf16[8,512,512]{2,1,0:T(8,128)(2,1)} %get-tuple-element.53, bf16[8,512,512]{2,1,0:T(8,128)(2,1)} %get-tuple-element.52), kind=kOutput, calls=%fused_computation.34 | convolution fusion | flops 2181038080 | bytes 14680064 | tf_op jit(solution)/shard_map/enm,emr->enr/dot_general | solution.py:308
  174.7 3.7 gather_fusion.7
  179.0 3.9 all-to-all-start.2
  182.9 7.6 %scatter_custom_fusion = f32[4096,128]{1,0:T(8,128)} fusion(s32[1024]{0:T(1024)S(1)} %bitcast.101, f32[1024,128]{1,0:T(8,128)S(1)} %bitcast.89, f32[]{:T(128)} %constant.113.clone.1), kind=kCustom, calls=%fused_computation.134 | custom fusion | flops 131072 | bytes 2097156 | tf_op jit(solution)/shard_map/scatter-add | solution.py:292
  193.7 57.5 %shard_map.123 = (f32[512,128]{1,0:T(8,128)S(1)}, f32[4,512,128]{2,1,0:T(8,128)S(1)}) custom-call(f32[8,512,128]{2,1,0:T(8,128)S(1)} %bitcast.69, f32[512,128]{1,0:T(8,128)S(1)} %multiply_subtract_fusion.2.refs_1_), custom_call_target="tpu_custom_call" | custom-call | flops 1000 | bytes 150000000 | tf_op jit(solution)/shard_map/pallas_call | solution.py:199
  252.1 7.6 %scatter_custom_fusion.2 = f32[4096,128]{1,0:T(8,128)} fusion(s32[1024]{0:T(1024)S(1)} %bitcast.102, f32[1024,128]{1,0:T(8,128)S(1)} %bitcast.92, f32[]{:T(128)} %constant.113.clone.1), kind=kCustom, calls=%fused_computation.130 | custom fusion | flops 131072 | bytes 2097156 | tf_op jit(solution)/shard_map/scatter-add | solution.py:292
  259.9 20.8 %fusion.2 = f32[4096,256]{1,0:T(8,128)} fusion(bf16[4096,2048]{1,0:T(8,128)(2,1)} %get-tuple-element.51, bf16[4096,2048]{1,0:T(8,128)(2,1)} %get-tuple-element.50, bf16[2048,128]{1,0:T(8,128)(2,1)} %get-tuple-element.63, bf16[2048,128]{1,0:T(8,128)(2,1)S(1)} %get-tuple-element.62), kind=kOutput, calls=%fused_computation.22 | convolution fusion | flops 8665432064 | bytes 38797312 | tf_op jit(solution)/shard_map/dot_general | solution.py:296
  283.8 53.5 %shard_map.124 = (f32[512,128]{1,0:T(8,128)S(1)}, f32[4,512,128]{2,1,0:T(8,128)S(1)}) custom-call(f32[8,512,128]{2,1,0:T(8,128)S(1)} %bitcast.70, f32[512,128]{1,0:T(8,128)S(1)} %multiply_subtract_fusion.1.refs_1_), custom_call_target="tpu_custom_call" | custom-call | flops 1000 | bytes 150000000 | tf_op jit(solution)/shard_map/pallas_call | solution.py:199
  348.8 20.2 %fusion.1 = f32[4096,256]{1,0:T(8,128)} fusion(bf16[4096,2048]{1,0:T(8,128)(2,1)} %get-tuple-element.51, bf16[4096,2048]{1,0:T(8,128)(2,1)} %get-tuple-element.50, bf16[2048,128]{1,0:T(8,128)(2,1)} %get-tuple-element.61, bf16[2048,128]{1,0:T(8,128)(2,1)S(1)} %copy-done.9), kind=kOutput, calls=%fused_computation.21 | convolution fusion | flops 8665432064 | bytes 38797312 | tf_op jit(solution)/shard_map/dot_general | solution.py:296
  369.2 5.0 %all-to-all-start.5 = ((f32[8,128,128]{2,1,0:T(8,128)}), f32[8,128,128]{2,1,0:T(8,128)S(1)}, u32[]{:S(2)}, u32[]{:S(2)}) async-start(f32[8,128,128]{2,1,0:T(8,128)} %get-tuple-element.66), calls=%async_computation.5 | async-start | bytes 1048576 | tf_op jit(solution)/shard_map/all_to_all | solution.py:302
  374.2 7.4 %scatter_custom_fusion.3 = f32[4096,128]{1,0:T(8,128)} fusion(s32[1024]{0:T(1024)S(1)} %bitcast.99, f32[1024,128]{1,0:T(8,128)S(1)} %bitcast.90, f32[]{:T(128)} %constant.113.clone.1), kind=kCustom, calls=%fused_computation.128 | custom fusion | flops 131072 | bytes 2097156 | tf_op jit(solution)/shard_map/scatter-add | solution.py:303
  381.6 3.9 fusion.39
  389.5 7.6 %scatter_custom_fusion.5 = f32[4096,128]{1,0:T(8,128)} fusion(s32[1024]{0:T(1024)S(1)} %bitcast.100, f32[1024,128]{1,0:T(8,128)S(1)} %bitcast.91, f32[]{:T(128)} %constant.113.clone.1), kind=kCustom, calls=%fused_computation.124 | custom fusion | flops 131072 | bytes 2097156 | tf_op jit(solution)/shard_map/scatter-add | solution.py:303
  406.4 9.0 %fusion.21 = f32[8,512,256]{2,1,0:T(8,128)} fusion(bf16[8,512,128]{2,1,0:T(8,128)(2,1)} %get-tuple-element.55, bf16[8,512,128]{2,1,0:T(8,128)(2,1)} %get-tuple-element.54, bf16[8,512,512]{2,1,0:T(8,128)(2,1)} %get-tuple-element.53, bf16[8,512,512]{2,1,0:T(8,128)(2,1)} %get-tuple-element.52), kind=kOutput, calls=%fused_computation.42 | convolution fusion | flops 2181038080 | bytes 14680064 | tf_op jit(solution)/shard_map/enm,emr->enr/dot_general | solution.py:308
  415.4 4.1 fusion.35
  419.4 3.7 gather_fusion.8
  424.8 6.7 %scatter_custom_fusion.4 = f32[4096,128]{1,0:T(8,128)S(1)} fusion(s32[1024]{0:T(1024)S(1)} %bitcast.103, f32[1024,128]{1,0:T(8,128)S(1)} %bitcast.88, f32[]{:T(128)} %constant.113.clone.1), kind=kCustom, calls=%fused_computation.126 | custom fusion | flops 131072 | bytes 2097156 | tf_op jit(solution)/shard_map/scatter-add | solution.py:292
  434.1 49.1 %shard_map.125 = f32[8,512,128]{2,1,0:T(8,128)S(1)} custom-call(f32[8,512,128]{2,1,0:T(8,128)S(1)} %bitcast.71, f32[512,128]{1,0:T(8,128)S(1)} %multiply_subtract_fusion.refs_1_), custom_call_target="tpu_custom_call" | custom-call | flops 1000 | bytes 150000000 | tf_op jit(solution)/shard_map/pallas_call | solution.py:199
  (142 shorter events, 70.7 us)
Async XLA Ops:
  0.6 8.4 %copy-start = (f32[4096,128]{1,0:T(8,128)S(1)}, f32[4096,128]{1,0:T(8,128)}, u32[]{:S(2)}) copy-start(f32[4096,128]{1,0:T(8,128)} %param.17) | copy-start | bytes 6291460
  45.0 11.5 %copy-start.10 = (s32[16384,1]{0,1:T(1,128)S(1)}, s32[16384,1]{0,1:T(1,128)}, u32[]{:S(2)}) copy-start(s32[16384,1]{0,1:T(1,128)} %param.23) | copy-start | bytes 196612
  45.0 12.4 %copy-start.11 = (s32[16384,1]{0,1:T(1,128)S(1)}, s32[16384,1]{0,1:T(1,128)}, u32[]{:S(2)}) copy-start(s32[16384,1]{0,1:T(1,128)} %param.25) | copy-start | bytes 196612
  46.0 93.0 %all-to-all-start.1 = ((f32[8,128,128]{2,1,0:T(8,128)}), f32[8,128,128]{2,1,0:T(8,128)S(1)}, u32[]{:S(2)}, u32[]{:S(2)}) async-start(f32[8,128,128]{2,1,0:T(8,128)} %broadcast_select_fusion.2), calls=%async_computation.1 | async-start | bytes 1048576 | tf_op jit(solution)/shard_map/all_to_all | solution.py:302
  51.2 84.1 %collective-permute-start = (f32[8,64,128]{2,1,0:T(8,128)}, f32[8,64,128]{2,1,0:T(8,128)S(1)}, u32[]{:S(2)}, u32[]{:S(2)}) collective-permute-start(f32[8,64,128]{2,1,0:T(8,128)} %slice.156), channel_id=1, source_target_pairs={{0,1},{1,2},{2,3},{3,4},{4,5},{5,6},{6,7},{7,8},{8,9},{9,10},{10,1... | collective-permute-start | bytes 786440 | tf_op jit(solution)/shard_map/ppermute | solution.py:21
  62.1 8.2 %copy-start.14 = (s32[8,64]{1,0:T(8,128)S(1)}, s32[8,64]{1,0:T(8,128)}, u32[]{:S(2)}) copy-start(s32[8,64]{1,0:T(8,128)} %param.27) | copy-start | bytes 6148
  62.1 9.8 %copy-start.12 = (s32[16384]{0:T(1024)S(1)}, s32[16384]{0:T(1024)}, u32[]{:S(2)}) copy-start(s32[16384]{0:T(1024)} %param.24) | copy-start | bytes 196612
  77.9 25.4 %copy-start.4 = (bf16[8,512,512]{2,1,0:T(8,128)(2,1)S(1)}, bf16[8,512,512]{2,1,0:T(8,128)(2,1)}, u32[]{:S(2)}) copy-start(bf16[8,512,512]{2,1,0:T(8,128)(2,1)} %get-tuple-element.52) | copy-start | bytes 12582916
  77.9 25.4 %copy-start.7 = (bf16[8,512,128]{2,1,0:T(8,128)(2,1)S(1)}, bf16[8,512,128]{2,1,0:T(8,128)(2,1)}, u32[]{:S(2)}) copy-start(bf16[8,512,128]{2,1,0:T(8,128)(2,1)} %get-tuple-element.59) | copy-start | bytes 3145732
  103.3 5.5 %copy-start.8 = (bf16[2048,128]{1,0:T(8,128)(2,1)S(1)}, bf16[2048,128]{1,0:T(8,128)(2,1)}, u32[]{:S(2)}) copy-start(bf16[2048,128]{1,0:T(8,128)(2,1)} %get-tuple-element.64) | copy-start | bytes 1572868
  129.2 6.0 %copy-start.5 = (f32[512,128]{1,0:T(8,128)S(1)}, f32[512,128]{1,0:T(8,128)}, u32[]{:S(2)}) copy-start(f32[512,128]{1,0:T(8,128)} %param.20) | copy-start | bytes 786436
  129.2 6.0 %copy-start.13 = (f32[512]{0:T(512)S(1)}, f32[512]{0:T(512)}, u32[]{:S(2)}) copy-start(f32[512]{0:T(512)} %param.19) | copy-start | bytes 6148
  150.6 2.0 copy-start.2
  158.3 20.7 %all-to-all-start = ((f32[4,256,128]{2,1,0:T(8,128)}), f32[4,256,128]{2,1,0:T(8,128)S(1)}, u32[]{:S(2)}, u32[]{:S(2)}) async-start(f32[4,256,128]{2,1,0:T(8,128)} %get-tuple-element.69), calls=%async_computation | async-start | bytes 1048576 | tf_op jit(solution)/shard_map/all_to_all | solution.py:291
  162.6 12.1 %collective-permute-start.1 = (f32[8,64,128]{2,1,0:T(8,128)S(1)}, f32[8,64,128]{2,1,0:T(8,128)S(1)}, u32[]{:S(2)}, u32[]{:S(2)}) collective-permute-start(f32[8,64,128]{2,1,0:T(8,128)S(1)} %slice.203), channel_id=1, source_target_pairs={{0,1},{1,2},{2,3},{3,4},{4,5},{5,6},{6,7},{7,8},{8,9},{9,10},{10,1... | collective-permute-start | bytes 786440 | tf_op jit(solution)/shard_map/ppermute | solution.py:21
  179.0 73.1 %all-to-all-start.2 = ((f32[4,256,128]{2,1,0:T(8,128)}), f32[4,256,128]{2,1,0:T(8,128)S(1)}, u32[]{:S(2)}, u32[]{:S(2)}) async-start(f32[4,256,128]{2,1,0:T(8,128)} %get-tuple-element.68), calls=%async_computation.2 | async-start | bytes 1048576 | tf_op jit(solution)/shard_map/all_to_all | solution.py:291
  341.3 7.5 %copy-start.9 = (bf16[2048,128]{1,0:T(8,128)(2,1)S(1)}, bf16[2048,128]{1,0:T(8,128)(2,1)}, u32[]{:S(2)}) copy-start(bf16[2048,128]{1,0:T(8,128)(2,1)} %get-tuple-element.60) | copy-start | bytes 1572868
  345.3 23.9 %all-to-all-start.3 = ((f32[8,128,128]{2,1,0:T(8,128)}), f32[8,128,128]{2,1,0:T(8,128)S(1)}, u32[]{:S(2)}, u32[]{:S(2)}) async-start(f32[8,128,128]{2,1,0:T(8,128)} %get-tuple-element.67), calls=%async_computation.3 | async-start | bytes 1048576 | tf_op jit(solution)/shard_map/all_to_all | solution.py:302
  369.2 20.4 %all-to-all-start.5 = ((f32[8,128,128]{2,1,0:T(8,128)}), f32[8,128,128]{2,1,0:T(8,128)S(1)}, u32[]{:S(2)}, u32[]{:S(2)}) async-start(f32[8,128,128]{2,1,0:T(8,128)} %get-tuple-element.66), calls=%async_computation.5 | async-start | bytes 1048576 | tf_op jit(solution)/shard_map/all_to_all | solution.py:302
  381.6 4.0 copy-start.6
  397.1 22.3 %collective-permute-start.2 = (f32[8,64,128]{2,1,0:T(8,128)S(1)}, f32[8,64,128]{2,1,0:T(8,128)S(1)}, u32[]{:S(2)}, u32[]{:S(2)}) collective-permute-start(f32[8,64,128]{2,1,0:T(8,128)S(1)} %slice.207), channel_id=1, source_target_pairs={{0,1},{1,2},{2,3},{3,4},{4,5},{5,6},{6,7},{7,8},{8,9},{9,10},{10,1... | collective-permute-start | bytes 786440 | tf_op jit(solution)/shard_map/ppermute | solution.py:21
  402.9 21.9 %all-to-all-start.4 = ((f32[4,256,128]{2,1,0:T(8,128)}), f32[4,256,128]{2,1,0:T(8,128)S(1)}, u32[]{:S(2)}, u32[]{:S(2)}) async-start(f32[4,256,128]{2,1,0:T(8,128)} %broadcast_select_fusion.3), calls=%async_computation.4 | async-start | bytes 1048576 | tf_op jit(solution)/shard_map/all_to_all | solution.py:291
  406.4 9.0 %copy-start.3 = (f32[4096,128]{1,0:T(8,128)S(1)}, f32[4096,128]{1,0:T(8,128)}, u32[]{:S(2)}) copy-start(f32[4096,128]{1,0:T(8,128)} %scatter_custom_fusion.5) | copy-start | bytes 6291460
  434.1 50.4 %copy-start.1 = (f32[4096,128]{1,0:T(8,128)S(1)}, f32[4096,128]{1,0:T(8,128)}, u32[]{:S(2)}) copy-start(f32[4096,128]{1,0:T(8,128)} %param.17) | copy-start | bytes 6291460

commit v3 on v2

--- a/solution.py
+++ b/solution.py
@@ -33,7 +33,9 @@
     stays = (target_row == r) & (target_col == c)
 
     if reduces:
-        partial, middle, refs = refs[0], refs[1], refs[2:]
+        panel_wide, trace_wide, trace_take, kernel, elem_mats, volume = refs[:6]
+        flux_wide, flux_take, face_wide, face_match, middle, volume_out = refs[6:12]
+        refs = refs[12:]
     else:
         middle, refs = refs[0], refs[1:]
     if finishes:
@@ -43,6 +45,8 @@
     if reduces:
         from_pair, summed_pair, from_line, refs = refs[0], refs[1], refs[2], refs[3:]
         pair_send, pair_recv, line_send, line_recv, refs = refs[0], refs[1], refs[2], refs[3], refs[4:]
+        partial, kernel_blocks, elem_blocks, kernel_sem, elem_sem = refs[:5]
+        refs = refs[5:]
     if finishes:
         out_send, out_recv, back_send, back_recv = refs
     else:
@@ -83,17 +87,66 @@
         )
 
     if reduces:
-        pair_copies = []
+        share_rows, columns = middle.shape
+        tile = min(128, share_rows)
+        elem_count, node_count, _ = volume.shape
+        face_count = face_match.shape[1]
+
+        def parts(block):
+            high = block.astype(jnp.bfloat16)
+            low = (block - high.astype(jnp.float32)).astype(jnp.bfloat16)
+            return high, low
+
+        def product(left, right):
+            return jnp.dot(left, right, preferred_element_type=jnp.float32)
+
+        def one_hot(hits):
+            return jnp.where(hits, 1.0, 0.0).astype(jnp.bfloat16)
+
+        def product_block(block, slot):
+            def step(t, carry):
+                rows = pl.ds(pl.multiple_of(t * tile, tile), tile)
+                high, low = parts(kernel_blocks[slot, rows, :])
+                place = lax.broadcasted_iota(jnp.int32, (tile, trace_wide.shape[1]), 0) + t * tile
+                wide = product(high, panel_wide[...]) + product(low, panel_wide[...])
+                wide -= product(one_hot(place == trace_take[block]), trace_wide[block])
+                partial[block, rows, :] = wide[:, :columns] + wide[:, columns:]
+                return carry
+
+            lax.fori_loop(0, share_rows // tile, step, 0)
+
+        def volume_step_of(e, carry):
+            field = volume[e]
+            high, low = parts(elem_blocks[e])
+            field_wide = jnp.concatenate(parts(field), axis=1)
+            wide = product(high, field_wide) + product(low, field_wide)
+            place = lax.broadcasted_iota(jnp.int32, (node_count, flux_wide.shape[0]), 0) + e * node_count
+            wide -= product(one_hot(place == flux_take[...]), flux_wide[...])
+            volume_out[e] = field - volume_step * (field + wide[:, :columns] + wide[:, columns:])
+            node = lax.broadcasted_iota(jnp.int32, (face_count, face_count), 1)
+            face = product(one_hot(node == face_match[e]), face_wide[e])
+            matched = face[:, :columns] + face[:, columns:]
+            volume_out[e, :face_count, :] += volume_step * face_weight * matched
+            return carry
+
+        elem_load = pltpu.make_async_copy(elem_mats, elem_blocks, elem_sem)
+        order = []
         for step in range(1, pairs + 1):
             other = (z + step) % pairs
-            copy = remote(
-                partial.at[other * 2 + (1 - h)], from_pair.at[step - 1],
-                pair_send.at[step - 1], pair_recv.at[step - 1], r, partner,
+            order += [other * 2 + (1 - h), other * 2 + h]
+
+        def load(i):
+            return pltpu.make_async_copy(
+                kernel.at[pl.ds(pl.multiple_of(order[i] * share_rows, share_rows), share_rows), :],
+                kernel_blocks.at[i % 2],
+                kernel_sem.at[i % 2],
             )
-            copy.start()
-            pair_copies.append(copy)
+
+        load(0).start()
+        pair_copies = []
         line_copies = []
-        for step in range(1, pairs):
+
+        def pass_on(step):
             other = (z + step) % pairs
             pair_copies[step - 1].wait_recv()
             summed_pair[step - 1] = from_pair[step - 1] + partial[other * 2 + h]
@@ -103,6 +156,24 @@
             )
             copy.start()
             line_copies.append(copy)
+
+        for i in range(2 * pairs):
+            if i + 1 < 2 * pairs:
+                load(i + 1).start()
+            load(i).wait()
+            product_block(order[i], i % 2)
+            if i % 2 == 0:
+                copy = remote(
+                    partial.at[order[i]], from_pair.at[i // 2],
+                    pair_send.at[i // 2], pair_recv.at[i // 2], r, partner,
+                )
+                copy.start()
+                pair_copies.append(copy)
+            elif i // 2 + 1 < pairs:
+                pass_on(i // 2 + 1)
+        elem_load.start()
+        elem_load.wait()
+        lax.fori_loop(0, elem_count // 2, volume_step_of, 0)
         pair_copies[pairs - 1].wait_recv()
         total = from_pair[pairs - 1] + partial[z * 2 + h]
         summed_pair[pairs - 1] = total
@@ -136,6 +207,8 @@
             )
             copy.start()
             back.append(copy)
+        if reduces:
+            lax.fori_loop(elem_count // 2, elem_count, volume_step_of, 0)
         for copy in back:
             copy.wait_recv()
         for copy in sent + back:
@@ -160,6 +233,8 @@
             )
             copy.start()
             sent.append(copy)
+        if reduces:
+            lax.fori_loop(elem_count // 2, elem_count, volume_step_of, 0)
         for copy in sent:
             copy.wait_recv()
         for copy in sent:
@@ -188,10 +263,21 @@
             jax.ShapeDtypeStruct((rows_n,) + block, jnp.float32),
         ]
     scratch = []
-    if reduces:
+    in_specs = [in_vmem] * len(operands)
+    if reduces:
+        kernel, elem_mats, volume = operands[3:6]
+        shapes = [jax.ShapeDtypeStruct(volume.shape, jnp.float32)] + shapes
+        in_specs[3] = in_specs[4] = pl.BlockSpec(memory_space=pl.ANY)
         scratch += [pltpu.VMEM((pairs,) + block, jnp.float32), pltpu.VMEM((pairs,) + block, jnp.float32)]
         scratch += [pltpu.VMEM((pairs - 1,) + block, jnp.float32)]
         scratch += [pltpu.SemaphoreType.DMA((pairs,))] * 2 + [pltpu.SemaphoreType.DMA((pairs - 1,))] * 2
+        scratch += [
+            pltpu.VMEM((cols_n,) + block, jnp.float32),
+            pltpu.VMEM((2, rows, kernel.shape[1]), jnp.float32),
+            pltpu.VMEM(elem_mats.shape, jnp.float32),
+            pltpu.SemaphoreType.DMA((2,)),
+            pltpu.SemaphoreType.DMA,
+        ]
     if finishes:
         scratch += [pltpu.SemaphoreType.DMA((pairs - 1,))] * 2 + [pltpu.SemaphoreType.DMA((pairs,))] * 2
     else:
@@ -199,11 +285,11 @@
     return pl.pallas_call(
         functools.partial(exchange_kernel, reduces, finishes),
         out_shape=shapes,
-        in_specs=[in_vmem] * len(operands),
+        in_specs=in_specs,
         out_specs=[in_vmem] * len(shapes),
         scratch_shapes=scratch,
         compiler_params=pltpu.CompilerParams(
-            collective_id=int(reduces) + int(finishes), has_side_effects=True, vmem_limit_bytes=24 << 20
+            collective_id=int(reduces) + int(finishes), has_side_effects=True, vmem_limit_bytes=(48 << 20) if reduces else (8 << 20)
         ),
         cost_estimate=pl.CostEstimate(flops=1000, bytes_accessed=150_000_000, transcendentals=0),
     )(*operands)
@@ -213,10 +299,6 @@
     high = lax.reduce_precision(block, 8, 7)
     low = block - high
     return jnp.concatenate([high.astype(jnp.bfloat16), low.astype(jnp.bfloat16)], axis=axis)
-
-
-def summed(wide, columns):
-    return wide[..., :columns] + wide[..., columns:]
 
 
 def block_plan(owner_blocks, slot_blocks, device_self, capacity):
@@ -261,25 +343,25 @@
     return_blocks = return_owner[:, 0].reshape(devices, share_rows)
     return_slots = return_slot.reshape(devices, share_rows)
 
-    trace_send, trace_send_ok = block_plan(trace_blocks, trace_slots, device_self, capacity)
+    trace_send, _ = block_plan(trace_blocks, trace_slots, device_self, capacity)
     own_trace = lax.dynamic_slice_in_dim(trace_blocks, row_index * col_devices, col_devices, 0)
-    block_places = jnp.arange(col_devices, dtype=jnp.int32)[:, None] * share_rows + positions[None, :]
-    trace_take = jax.vmap(lambda r: block_plan(own_trace, block_places, r * col_devices + col_index, capacity)[0])(
-        jnp.arange(row_devices, dtype=jnp.int32)
-    )
+    own_places = jnp.broadcast_to(positions[None, :], (col_devices, share_rows))
+    trace_take, trace_take_ok = jax.vmap(
+        lambda r: block_plan(own_trace, own_places, r * col_devices + col_index, capacity)
+    )(jnp.arange(row_devices, dtype=jnp.int32))
+    trace_take = jnp.where(trace_take_ok, trace_take, -1).transpose(1, 0, 2)
+    trace_take = trace_take.reshape(col_devices, 1, row_devices * capacity)
     own_return = lax.dynamic_slice_in_dim(return_blocks, col_index * row_devices, row_devices, 0)
     panel_places = jnp.arange(row_devices, dtype=jnp.int32)[:, None] * share_rows + positions[None, :]
-    flux_send, flux_send_ok = jax.vmap(
-        lambda d: block_plan(own_return, panel_places, row_index * col_devices + d, capacity)
+    flux_send = jax.vmap(
+        lambda d: block_plan(own_return, panel_places, row_index * col_devices + d, capacity)[0]
     )(jnp.arange(col_devices, dtype=jnp.int32))
-    flux_take, _ = block_plan(return_blocks, return_slots, device_self, capacity)
+    flux_take, flux_take_ok = block_plan(return_blocks, return_slots, device_self, capacity)
     slots = devices * capacity
-    trace_send, trace_send_ok = trace_send.reshape(slots), trace_send_ok.reshape(slots, 1)
-    flux_send, flux_send_ok = flux_send.reshape(slots), flux_send_ok.reshape(slots, 1)
-    trace_take, flux_take = trace_take.reshape(slots), flux_take.reshape(slots)
-
-    kernel_halves = halves(kernel, 1)
-    elem_halves = halves(elem_mats, 2)
+    trace_send, flux_send = trace_send.reshape(slots), flux_send.reshape(slots)
+    flux_take = jnp.where(flux_take_ok, flux_take, -1).reshape(1, slots)
+    face_rows = face_match[:, :, None]
+
     share = lax.dynamic_slice_in_dim(boundary_start, col_index * share_rows, share_rows, 0)
     share, panel = exchange(False, False, share)
     volume_field = volume_start
@@ -287,38 +369,22 @@
         panel = panel.reshape(row_devices * share_rows, columns)
 
         volume_flat = volume_field.reshape(elem_count * node_count, columns)
-        outgoing = jnp.where(trace_send_ok, volume_flat[trace_send], 0.0)
+        outgoing = jnp.take(volume_flat, trace_send, axis=0, mode="clip")
         arrived = lax.all_to_all(outgoing, "row", split_axis=0, concat_axis=0, tiled=True)
-        traced = jnp.zeros((row_panel, columns), jnp.float32).at[trace_take].add(arrived)
-
-        wide = halves(panel, 1)
-        image = summed(
-            jnp.dot(kernel_halves, jnp.concatenate([wide, wide], 0), preferred_element_type=jnp.float32),
-            columns,
+        arrived = arrived.reshape(row_devices, col_devices, capacity, columns).transpose(1, 0, 2, 3)
+        trace_wide = halves(arrived.reshape(col_devices, row_devices * capacity, columns), 2)
+        leaving = jnp.take(panel, flux_send, axis=0, mode="clip")
+        landed = lax.all_to_all(leaving, "col", split_axis=0, concat_axis=0, tiled=True)
+        lower_faces = passed_along(volume_field[:, node_count - face_count :, :], ("row", "col"), 1)
+        middle = share - boundary_step * (diag_part[:, None] * share - incident)
+        operands = (
+            halves(panel, 1), trace_wide, trace_take, kernel, elem_mats, volume_field,
+            halves(landed, 1), flux_take, halves(lower_faces, 2), face_rows, middle,
         )
-        partial_value = (image - traced).reshape(col_devices, share_rows, columns)
-        middle = share - boundary_step * (diag_part[:, None] * share - incident)
-        leaving = jnp.where(flux_send_ok, panel[flux_send], 0.0)
-        landed = lax.all_to_all(leaving, "col", split_axis=0, concat_axis=0, tiled=True)
-        flux_field = jnp.zeros_like(volume_flat).at[flux_take].add(landed).reshape(volume_field.shape)
-        lower_faces = passed_along(volume_field[:, node_count - face_count :, :], ("row", "col"), 1)
-        matched = jax.vmap(lambda face_rows, face_order: face_rows[face_order])(lower_faces, face_match)
-        volume_wide = halves(volume_field, 2)
-        applied = summed(
-            jnp.einsum(
-                "enm,emr->enr",
-                elem_halves,
-                jnp.concatenate([volume_wide, volume_wide], 1),
-                preferred_element_type=jnp.float32,
-            ),
-            columns,
-        )
-        updated = volume_field - volume_step * (volume_field + applied - flux_field)
-        volume_field = updated.at[:, :face_count, :].add(volume_step * face_weight * matched)
         if sweep_index < ITERS - 1:
-            share, panel = exchange(True, False, partial_value, middle)
+            volume_field, share, panel = exchange(True, False, *operands)
         else:
-            (boundary_final,) = exchange(True, True, partial_value, middle)
+            volume_field, boundary_final = exchange(True, True, *operands)
     return (boundary_final.reshape(row_panel, columns), volume_field)
 
 

time: 491 us -> 368 us (0.75)
  other arithmetic: 136 us -> 25.7 us
  matrix products: 84.6 us -> 0 us
  waiting for transfers between devices: 2.06 us -> 44.8 us
  Pallas kernels: 192 us -> 214 us
  local copies, waits for them, and re-layouts: 37.5 us -> 44.6 us
    dot_general x6 -> x0, matrix products: 84.6 us -> none  [the longest x3 61.3 us: shards(): jnp.dot(kernel_halves, jnp.concatenate([wide, wide], 0), preferred_elemen...]
    scatter-add x9 -> x0, other arithmetic: 46.4 us -> none  [the longest x3 22.6 us: shards(): jnp.zeros_like(volume_flat).at[flux_take].add(landed)]
    convert_element_type x8 -> x12, other arithmetic: 43.7 us -> 4.06 us  [halves(): high.astype(jnp.bfloat16)]
    all_to_all x3, waiting for transfers between devices: 2.05 us -> 40.5 us  [shards(): lax.all_to_all(leaving, 'col', split_axis=0, concat_axis=0, tiled=True)]
    pallas_call x4, Pallas kernels: 192 us -> 214 us  [exchange(): pl.pallas_call(functools.partial(exchange_kernel, reduces, finishes), out...]
    sub x6 -> x0, other arithmetic: 20.8 us -> none  [the longest x3 11.9 us: shards(): updated = volume_field - volume_step * (volume_field + applied - flux_field)]
    gather x10 -> x6, local copies, waits for them, and re-layouts: 31.1 us -> 29 us  [the longest x3 16.9 us: shards(): outgoing = jnp.take(volume_flat, trace_send, axis=0, mode='clip')]
  transfers between devices with their start and end apart: 9 -> 9, of which waited for: 1 -> 5; matrix products, arithmetic and copies ran while one was open for 35% -> 16% of each run, Pallas kernels for 12% -> 9%
where the time goes in v3:
time: 368 us; the launch traced here: 362 us
  Pallas kernels  214 us (58%)
  waiting for transfers between devices  44.8 us (12%)
  local copies, waits for them, and re-layouts  44.6 us (12%)
  starting transfers between devices  31.5 us (9%)
  other arithmetic  25.7 us (7%)
    pallas_call x4, Pallas kernels, exchange(): pl.pallas_call(functools.partial(exchange_kernel, reduces, finishes), out...  214 us
    all_to_all x3, waiting for transfers between devices, shards(): lax.all_to_all(leaving, 'col', split_axis=0, concat_axis=0, tiled=True)  40.5 us
    gather x3, local copies, waits for them, and re-layouts, shards(): outgoing = jnp.take(volume_flat, trace_send, axis=0, mode='clip')  16.9 us
    all_to_all x3, starting transfers between devices, shards(): lax.all_to_all(leaving, 'col', split_axis=0, concat_axis=0, tiled=True)  12.6 us
    gather x3, local copies, waits for them, and re-layouts, shards(): leaving = jnp.take(panel, flux_send, axis=0, mode='clip')  12.1 us
    all_to_all x3, starting transfers between devices, shards(): lax.all_to_all(outgoing, 'row', split_axis=0, concat_axis=0, tiled=True)  11.9 us
    another operation x8, other arithmetic  11.5 us
  transfers between devices with their start and end apart: 9, of which 5 were waited for; matrix products, arithmetic and copies ran while one was open for 16% of the time, Pallas kernels for 9%

profile of v3, /device:TPU:0, one launch (start us, length us, event | category | flops | bytes accessed | tf_op | source)
XLA Modules:
  0.0 362.4 jit_solution(16918431340391461843)
XLA Ops:
  0.6 1.8 slice.41
  2.5 3.1 collective-permute-start
  6.9 1.6 reduce.12
  8.6 1.6 reduce.13
  13.6 5.7 %gather_fusion = f32[1024,128]{1,0:T(8,128)} fusion(f32[4096,128]{1,0:T(8,128)} %bitcast.73, s32[1024]{0:T(1024)S(1)} %broadcast_clamp_fusion.1), kind=kCustom, calls=%fused_computation | custom fusion | bytes 1052672 | tf_op jit(solution)/shard_map/jit(_take)/gather | solution.py:372
  19.2 4.0 %all-to-all-start = ((f32[4,256,128]{2,1,0:T(8,128)}), f32[4,256,128]{2,1,0:T(8,128)S(1)}, u32[]{:S(2)}, u32[]{:S(2)}) async-start(f32[4,256,128]{2,1,0:T(8,128)} %bitcast.3), calls=%async_computation | async-start | bytes 1048576 | tf_op jit(solution)/shard_map/all_to_all | solution.py:373
  23.5 4.5 %reduce-window.30 = s32[4,8,4,128]{3,1,2,0:T(8,128)S(1)} reduce-window(s32[4,8,4,128]{3,1,2,0:T(8,128)S(1)} %compare_convert_fusion.3, s32[]{:T(128)} %constant.16.clone.1), window={size=1x1x1x128 pad=0_0x0_0x0_0x127_0}, to_apply=%region_3.4 | reduce-window | flops 2080768 | bytes 131076 | tf_op jit(solution)/shard_map/reduce-window.2
  30.1 4.5 %reduce-window.34 = s32[8,4,4,128]{3,0,1,2:T(8,128)S(1)} reduce-window(s32[8,4,4,128]{3,0,1,2:T(8,128)S(1)} %compare_convert_fusion.2, s32[]{:T(128)} %constant.16.clone.1), window={size=1x1x1x128 pad=0_0x0_0x0_0x127_0}, to_apply=%region_7.8 | reduce-window | flops 2080768 | bytes 131076 | tf_op jit(solution)/shard_map/reduce-window.4
  38.7 32.4 %shard_map.122 = (f32[512,128]{1,0:T(8,128)S(1)}, f32[4,512,128]{2,1,0:T(8,128)S(1)}) custom-call(f32[512,128]{1,0:T(8,128)S(1)} %constant_dynamic-slice_fusion.2.refs_0_), custom_call_target="tpu_custom_call" | custom-call | flops 1000 | bytes 150000000 | tf_op jit(solution)/shard_map/pallas_call | solution.py:285
  72.0 4.0 %gather_fusion.1 = f32[1024,128]{1,0:T(8,128)} fusion(f32[2048,128]{1,0:T(8,128)S(1)} %bitcast.72, s32[1024]{0:T(1024)S(1)} %broadcast_clamp_fusion), kind=kCustom, calls=%fused_computation.1 | custom fusion | bytes 1052672 | tf_op jit(solution)/shard_map/jit(_take)/gather | solution.py:376
  76.0 3.5 all-to-all-start.1
  81.0 13.8 %all-to-all-done.1 = f32[8,128,128]{2,1,0:T(8,128)S(1)} async-done(((f32[8,128,128]{2,1,0:T(8,128)}), f32[8,128,128]{2,1,0:T(8,128)S(1)}, u32[]{:S(2)}, u32[]{:S(2)}) %all-to-all-start.1) | async-done | bytes 524320 | tf_op jit(solution)/shard_map/all_to_all | solution.py:377
  94.9 63.2 %shard_map.123 = (f32[8,512,128]{2,1,0:T(8,128)}, f32[512,128]{1,0:T(8,128)S(1)}, f32[4,512,128]{2,1,0:T(8,128)S(1)}) custom-call(bf16[2048,256]{1,0:T(8,128)(2,1)S(1)} %pad_maximum_fusion.refs_0_, bf16[8,128,256]{2,1,0:T(8,128)(2,1)S(1)} %pad_maximum_fusion.3.refs_1_, s32[8,1,128]{2,1,0:T(1,128)S(1)} %reshape.221.refs_2_, f32[4096,2048]{1,0:T(8,128)} %refs_3_.5, ...), custom_call_target="tpu_custom_call" | custom-call | flops 1000 | bytes 150000000 | tf_op jit(solution)/shard_map/pallas_call | solution.py:285
  158.9 1.7 slice.42
  160.5 2.0 collective-permute-start.1
  162.5 5.6 %gather_fusion.2 = f32[1024,128]{1,0:T(8,128)} fusion(f32[4096,128]{1,0:T(8,128)} %bitcast.75, s32[1024]{0:T(1024)S(1)} %broadcast_clamp_fusion.1), kind=kCustom, calls=%fused_computation.2 | custom fusion | bytes 1052672 | tf_op jit(solution)/shard_map/jit(_take)/gather | solution.py:372
  168.1 3.5 all-to-all-start.2
  171.9 4.0 %gather_fusion.3 = f32[1024,128]{1,0:T(8,128)} fusion(f32[2048,128]{1,0:T(8,128)S(1)} %bitcast.71, s32[1024]{0:T(1024)S(1)} %broadcast_clamp_fusion), kind=kCustom, calls=%fused_computation.3 | custom fusion | bytes 1052672 | tf_op jit(solution)/shard_map/jit(_take)/gather | solution.py:376
  176.0 2.2 all-to-all-done.2
  178.1 4.6 %all-to-all-start.3 = ((f32[8,128,128]{2,1,0:T(8,128)}), f32[8,128,128]{2,1,0:T(8,128)S(1)}, u32[]{:S(2)}, u32[]{:S(2)}) async-start(f32[8,128,128]{2,1,0:T(8,128)} %bitcast.81), calls=%async_computation.3 | async-start | bytes 1048576 | tf_op jit(solution)/shard_map/all_to_all | solution.py:377
  184.2 13.9 %all-to-all-done.3 = f32[8,128,128]{2,1,0:T(8,128)S(1)} async-done(((f32[8,128,128]{2,1,0:T(8,128)}), f32[8,128,128]{2,1,0:T(8,128)S(1)}, u32[]{:S(2)}, u32[]{:S(2)}) %all-to-all-start.3) | async-done | bytes 524320 | tf_op jit(solution)/shard_map/all_to_all | solution.py:377
  198.2 62.9 %shard_map.124 = (f32[8,512,128]{2,1,0:T(8,128)}, f32[512,128]{1,0:T(8,128)S(1)}, f32[4,512,128]{2,1,0:T(8,128)S(1)}) custom-call(bf16[2048,256]{1,0:T(8,128)(2,1)S(1)} %pad_maximum_fusion.1.refs_0_, bf16[8,128,256]{2,1,0:T(8,128)(2,1)S(1)} %pad_maximum_fusion.5.refs_1_, s32[8,1,128]{2,1,0:T(1,128)S(1)} %reshape.221.refs_2_, f32[4096,2048]{1,0:T(8,128)} %refs_3_.5, ...), custom_call_target="tpu_custom_call" | custom-call | flops 1000 | bytes 150000000 | tf_op jit(solution)/shard_map/pallas_call | solution.py:285
  261.8 1.7 slice.43
  263.5 2.0 collective-permute-start.2
  265.5 5.6 %gather_fusion.4 = f32[1024,128]{1,0:T(8,128)} fusion(f32[4096,128]{1,0:T(8,128)} %bitcast.74, s32[1024]{0:T(1024)S(1)} %broadcast_clamp_fusion.1), kind=kCustom, calls=%fused_computation.4 | custom fusion | bytes 1052672 | tf_op jit(solution)/shard_map/jit(_take)/gather | solution.py:372
  271.1 4.4 %all-to-all-start.4 = ((f32[4,256,128]{2,1,0:T(8,128)}), f32[4,256,128]{2,1,0:T(8,128)}, u32[]{:S(2)}, u32[]{:S(2)}) async-start(f32[4,256,128]{2,1,0:T(8,128)} %bitcast.26), calls=%async_computation.4 | async-start | bytes 1048576 | tf_op jit(solution)/shard_map/all_to_all | solution.py:373
  275.8 4.0 %gather_fusion.5 = f32[1024,128]{1,0:T(8,128)} fusion(f32[2048,128]{1,0:T(8,128)S(1)} %bitcast.70, s32[1024]{0:T(1024)S(1)} %broadcast_clamp_fusion), kind=kCustom, calls=%fused_computation.5 | custom fusion | bytes 1052672 | tf_op jit(solution)/shard_map/jit(_take)/gather | solution.py:376
  279.8 2.1 all-to-all-done.4
  281.9 4.5 %all-to-all-start.5 = ((f32[8,128,128]{2,1,0:T(8,128)}), f32[8,128,128]{2,1,0:T(8,128)S(1)}, u32[]{:S(2)}, u32[]{:S(2)}) async-start(f32[8,128,128]{2,1,0:T(8,128)} %bitcast.79), calls=%async_computation.5 | async-start | bytes 1048576 | tf_op jit(solution)/shard_map/all_to_all | solution.py:377
  288.9 12.8 %all-to-all-done.5 = f32[8,128,128]{2,1,0:T(8,128)S(1)} async-done(((f32[8,128,128]{2,1,0:T(8,128)}), f32[8,128,128]{2,1,0:T(8,128)S(1)}, u32[]{:S(2)}, u32[]{:S(2)}) %all-to-all-start.5) | async-done | bytes 524320 | tf_op jit(solution)/shard_map/all_to_all | solution.py:377
  301.9 55.9 %shard_map.125 = (f32[8,512,128]{2,1,0:T(8,128)S(1)}, f32[8,512,128]{2,1,0:T(8,128)}) custom-call(bf16[2048,256]{1,0:T(8,128)(2,1)S(1)} %pad_maximum_fusion.2.refs_0_, bf16[8,128,256]{2,1,0:T(8,128)(2,1)S(1)} %pad_maximum_fusion.7.refs_1_, s32[8,1,128]{2,1,0:T(1,128)S(1)} %reshape.221.refs_2_, f32[4096,2048]{1,0:T(8,128)} %refs_3_.5, ...), custom_call_target="tpu_custom_call" | custom-call | flops 1000 | bytes 150000000 | tf_op jit(solution)/shard_map/pallas_call | solution.py:285
  357.9 3.2 copy.54
  (127 shorter events, 20.7 us)
Async XLA Ops:
  0.6 37.3 %copy-start = (f32[4096,128]{1,0:T(8,128)S(1)}, f32[4096,128]{1,0:T(8,128)}, u32[]{:S(2)}) copy-start(f32[4096,128]{1,0:T(8,128)} %param.11) | copy-start | bytes 6291460
  2.5 77.2 %collective-permute-start = (f32[8,64,128]{2,1,0:T(8,128)}, f32[8,64,128]{2,1,0:T(8,128)}, u32[]{:S(2)}, u32[]{:S(2)}) collective-permute-start(f32[8,64,128]{2,1,0:T(8,128)} %slice.41), channel_id=1, source_target_pairs={{0,1},{1,2},{2,3},{3,4},{4,5},{5,6},{6,7},{7,8},{8,9},{9,10},{10,1... | collective-permute-start | bytes 786440 | tf_op jit(solution)/shard_map/ppermute | solution.py:21
  13.6 16.4 %copy-start.13 = (s32[16384]{0:T(1024)S(1)}, s32[16384]{0:T(1024)}, u32[]{:S(2)}) copy-start(s32[16384]{0:T(1024)} %param.20) | copy-start | bytes 196612
  19.2 56.8 %all-to-all-start = ((f32[4,256,128]{2,1,0:T(8,128)}), f32[4,256,128]{2,1,0:T(8,128)S(1)}, u32[]{:S(2)}, u32[]{:S(2)}) async-start(f32[4,256,128]{2,1,0:T(8,128)} %bitcast.3), calls=%async_computation | async-start | bytes 1048576 | tf_op jit(solution)/shard_map/all_to_all | solution.py:373
  71.1 0.7 copy-start.15
  72.0 7.6 %copy-start.6 = (f32[512,128]{1,0:T(8,128)S(1)}, f32[512,128]{1,0:T(8,128)}, u32[]{:S(2)}) copy-start(f32[512,128]{1,0:T(8,128)} %param.14) | copy-start | bytes 786436
  72.0 7.6 %copy-start.14 = (f32[512]{0:T(512)S(1)}, f32[512]{0:T(512)}, u32[]{:S(2)}) copy-start(f32[512]{0:T(512)} %param.13) | copy-start | bytes 6148
  76.0 3.5 copy-start.9
  76.0 18.8 %all-to-all-start.1 = ((f32[8,128,128]{2,1,0:T(8,128)}), f32[8,128,128]{2,1,0:T(8,128)S(1)}, u32[]{:S(2)}, u32[]{:S(2)}) async-start(f32[8,128,128]{2,1,0:T(8,128)} %bitcast.80), calls=%async_computation.1 | async-start | bytes 1048576 | tf_op jit(solution)/shard_map/all_to_all | solution.py:377
  79.6 1.2 copy-start.10
  158.2 0.7 copy-start.4
  160.5 22.4 %collective-permute-start.1 = (f32[8,64,128]{2,1,0:T(8,128)}, f32[8,64,128]{2,1,0:T(8,128)}, u32[]{:S(2)}, u32[]{:S(2)}) collective-permute-start(f32[8,64,128]{2,1,0:T(8,128)} %slice.42), channel_id=1, source_target_pairs={{0,1},{1,2},{2,3},{3,4},{4,5},{5,6},{6,7},{7,8},{8,9},{9,10},{10,1... | collective-permute-start | bytes 786440 | tf_op jit(solution)/shard_map/ppermute | solution.py:21
  168.1 10.0 %all-to-all-start.2 = ((f32[4,256,128]{2,1,0:T(8,128)}), f32[4,256,128]{2,1,0:T(8,128)S(1)}, u32[]{:S(2)}, u32[]{:S(2)}) async-start(f32[4,256,128]{2,1,0:T(8,128)} %bitcast.18), calls=%async_computation.2 | async-start | bytes 1048576 | tf_op jit(solution)/shard_map/all_to_all | solution.py:373
  171.9 10.8 %copy-start.5 = (f32[512,128]{1,0:T(8,128)S(1)}, f32[512,128]{1,0:T(8,128)}, u32[]{:S(2)}) copy-start(f32[512,128]{1,0:T(8,128)} %copy-done.4) | copy-start | bytes 786436
  171.9 10.8 %copy-start.7 = (f32[512,128]{1,0:T(8,128)S(1)}, f32[512,128]{1,0:T(8,128)}, u32[]{:S(2)}) copy-start(f32[512,128]{1,0:T(8,128)} %param.14) | copy-start | bytes 786436
  178.1 4.6 %copy-start.11 = (f32[4,256,128]{2,1,0:T(8,128)}, f32[4,256,128]{2,1,0:T(8,128)S(1)}, u32[]{:S(2)}) copy-start(f32[4,256,128]{2,1,0:T(8,128)S(1)} %all-to-all-done.2) | copy-start | bytes 1572868
  178.1 19.9 %all-to-all-start.3 = ((f32[8,128,128]{2,1,0:T(8,128)}), f32[8,128,128]{2,1,0:T(8,128)S(1)}, u32[]{:S(2)}, u32[]{:S(2)}) async-start(f32[8,128,128]{2,1,0:T(8,128)} %bitcast.81), calls=%async_computation.3 | async-start | bytes 1048576 | tf_op jit(solution)/shard_map/all_to_all | solution.py:377
  182.8 1.2 copy-start.12
  261.1 0.7 copy-start.2
  263.5 23.1 %collective-permute-start.2 = (f32[8,64,128]{2,1,0:T(8,128)}, f32[8,64,128]{2,1,0:T(8,128)}, u32[]{:S(2)}, u32[]{:S(2)}) collective-permute-start(f32[8,64,128]{2,1,0:T(8,128)} %slice.43), channel_id=1, source_target_pairs={{0,1},{1,2},{2,3},{3,4},{4,5},{5,6},{6,7},{7,8},{8,9},{9,10},{10,1... | collective-permute-start | bytes 786440 | tf_op jit(solution)/shard_map/ppermute | solution.py:21
  271.1 10.8 %all-to-all-start.4 = ((f32[4,256,128]{2,1,0:T(8,128)}), f32[4,256,128]{2,1,0:T(8,128)}, u32[]{:S(2)}, u32[]{:S(2)}) async-start(f32[4,256,128]{2,1,0:T(8,128)} %bitcast.26), calls=%async_computation.4 | async-start | bytes 1048576 | tf_op jit(solution)/shard_map/all_to_all | solution.py:373
  275.8 10.7 %copy-start.3 = (f32[512,128]{1,0:T(8,128)S(1)}, f32[512,128]{1,0:T(8,128)}, u32[]{:S(2)}) copy-start(f32[512,128]{1,0:T(8,128)} %copy-done.2) | copy-start | bytes 786436
  275.8 10.7 %copy-start.8 = (f32[512,128]{1,0:T(8,128)S(1)}, f32[512,128]{1,0:T(8,128)}, u32[]{:S(2)}) copy-start(f32[512,128]{1,0:T(8,128)} %param.14) | copy-start | bytes 786436
  281.9 19.8 %all-to-all-start.5 = ((f32[8,128,128]{2,1,0:T(8,128)}), f32[8,128,128]{2,1,0:T(8,128)S(1)}, u32[]{:S(2)}, u32[]{:S(2)}) async-start(f32[8,128,128]{2,1,0:T(8,128)} %bitcast.79), calls=%async_computation.5 | async-start | bytes 1048576 | tf_op jit(solution)/shard_map/all_to_all | solution.py:377
  357.9 4.5 %copy-start.1 = (f32[4096,128]{1,0:T(8,128)S(1)}, f32[4096,128]{1,0:T(8,128)}, u32[]{:S(2)}) copy-start(f32[4096,128]{1,0:T(8,128)} %param.11) | copy-start | bytes 6291460

commit v4 on v3

--- a/solution.py
+++ b/solution.py
@@ -34,7 +34,7 @@
 
     if reduces:
         panel_wide, trace_wide, trace_take, kernel, elem_mats, volume = refs[:6]
-        flux_wide, flux_take, face_wide, face_match, middle, volume_out = refs[6:12]
+        flux_send, flux_take, face_wide, face_match, middle, volume_out = refs[6:12]
         refs = refs[12:]
     else:
         middle, refs = refs[0], refs[1:]
@@ -46,7 +46,8 @@
         from_pair, summed_pair, from_line, refs = refs[0], refs[1], refs[2], refs[3:]
         pair_send, pair_recv, line_send, line_recv, refs = refs[0], refs[1], refs[2], refs[3], refs[4:]
         partial, kernel_blocks, elem_blocks, kernel_sem, elem_sem = refs[:5]
-        refs = refs[5:]
+        leaving, landed, flux_wide, flux_out, flux_in = refs[5:10]
+        refs = refs[10:]
     if finishes:
         out_send, out_recv, back_send, back_recv = refs
     else:
@@ -59,10 +60,9 @@
 
     greeted = 0
     if reduces:
-        greet(r, partner)
-        for step in range(1, pairs):
-            greet(r, ((z + step) % pairs) * 2 + h)
-        greeted += pairs
+        for step in range(1, cols_n):
+            greet(r, (c + step) % cols_n)
+        greeted += cols_n - 1
     if not finishes:
         for step in range(1, rows_n):
             greet((r + step) % rows_n, c)
@@ -143,6 +143,23 @@
             )
 
         load(0).start()
+        elem_load.start()
+
+        def picked(member):
+            node = lax.broadcasted_iota(jnp.int32, (flux_send.shape[1], panel_wide.shape[0]), 1)
+            wide = product(one_hot(node == flux_send[member]), panel_wide[...])
+            return wide[:, :columns] + wide[:, columns:]
+
+        flux_copies = []
+        for step in range(1, cols_n):
+            member = (c + step) % cols_n
+            leaving[step - 1] = picked(member)
+            copy = remote(
+                leaving.at[step - 1], landed.at[c], flux_out.at[step - 1], flux_in.at[step - 1], r, member
+            )
+            copy.start()
+            flux_copies.append(copy)
+        landed[c] = picked(c)
         pair_copies = []
         line_copies = []
 
@@ -171,8 +188,10 @@
                 pair_copies.append(copy)
             elif i // 2 + 1 < pairs:
                 pass_on(i // 2 + 1)
-        elem_load.start()
         elem_load.wait()
+        for copy in flux_copies:
+            copy.wait_recv()
+        flux_wide[...] = jnp.concatenate(parts(landed[...].reshape(flux_wide.shape[0], columns)), axis=1)
         lax.fori_loop(0, elem_count // 2, volume_step_of, 0)
         pair_copies[pairs - 1].wait_recv()
         total = from_pair[pairs - 1] + partial[z * 2 + h]
@@ -245,7 +264,7 @@
             move.wait_send()
 
     if reduces:
-        for copy in pair_copies + line_copies:
+        for copy in pair_copies + line_copies + flux_copies:
             copy.wait_send()
 
 
@@ -278,6 +297,13 @@
             pltpu.SemaphoreType.DMA((2,)),
             pltpu.SemaphoreType.DMA,
         ]
+        slots = operands[6].shape[1]
+        scratch += [
+            pltpu.VMEM((cols_n - 1, slots, columns), jnp.float32),
+            pltpu.VMEM((cols_n, slots, columns), jnp.float32),
+            pltpu.VMEM((cols_n * slots, 2 * columns), jnp.bfloat16),
+        ]
+        scratch += [pltpu.SemaphoreType.DMA((cols_n - 1,))] * 2
     if finishes:
         scratch += [pltpu.SemaphoreType.DMA((pairs - 1,))] * 2 + [pltpu.SemaphoreType.DMA((pairs,))] * 2
     else:
@@ -358,7 +384,8 @@
     )(jnp.arange(col_devices, dtype=jnp.int32))
     flux_take, flux_take_ok = block_plan(return_blocks, return_slots, device_self, capacity)
     slots = devices * capacity
-    trace_send, flux_send = trace_send.reshape(slots), flux_send.reshape(slots)
+    trace_send = trace_send.reshape(slots)
+    flux_send = flux_send.reshape(col_devices, row_devices * capacity, 1)
     flux_take = jnp.where(flux_take_ok, flux_take, -1).reshape(1, slots)
     face_rows = face_match[:, :, None]
 
@@ -373,13 +400,11 @@
         arrived = lax.all_to_all(outgoing, "row", split_axis=0, concat_axis=0, tiled=True)
         arrived = arrived.reshape(row_devices, col_devices, capacity, columns).transpose(1, 0, 2, 3)
         trace_wide = halves(arrived.reshape(col_devices, row_devices * capacity, columns), 2)
-        leaving = jnp.take(panel, flux_send, axis=0, mode="clip")
-        landed = lax.all_to_all(leaving, "col", split_axis=0, concat_axis=0, tiled=True)
         lower_faces = passed_along(volume_field[:, node_count - face_count :, :], ("row", "col"), 1)
         middle = share - boundary_step * (diag_part[:, None] * share - incident)
         operands = (
             halves(panel, 1), trace_wide, trace_take, kernel, elem_mats, volume_field,
-            halves(landed, 1), flux_take, halves(lower_faces, 2), face_rows, middle,
+            flux_send, flux_take, halves(lower_faces, 2), face_rows, middle,
         )
         if sweep_index < ITERS - 1:
             volume_field, share, panel = exchange(True, False, *operands)

time: 368 us -> 326 us (0.89)
  waiting for transfers between devices: 44.8 us -> 8.15 us
  Pallas kernels: 214 us -> 234 us
  local copies, waits for them, and re-layouts: 44.6 us -> 30.3 us
  starting transfers between devices: 31.5 us -> 18.3 us
    all_to_all x3 -> x0, waiting for transfers between devices: 40.5 us -> none  [shards(): lax.all_to_all(leaving, 'col', split_axis=0, concat_axis=0, tiled=True)]
    pallas_call x4, Pallas kernels: 214 us -> 234 us  [exchange(): pl.pallas_call(functools.partial(exchange_kernel, reduces, finishes), out...]
    all_to_all x3 -> x0, starting transfers between devices: 12.6 us -> none  [shards(): lax.all_to_all(leaving, 'col', split_axis=0, concat_axis=0, tiled=True)]
    gather x3 -> x0, local copies, waits for them, and re-layouts: 12.1 us -> none  [shards(): leaving = jnp.take(panel, flux_send, axis=0, mode='clip')]
    all_to_all x3, waiting for transfers between devices: 4.29 us -> 8.14 us  [shards(): lax.all_to_all(outgoing, 'row', split_axis=0, concat_axis=0, tiled=True)]
  transfers between devices with their start and end apart: 9 -> 6, of which waited for: 5 -> 2; matrix products, arithmetic and copies ran while one was open for 16% -> 15% of each run, Pallas kernels for 9% -> 10%
where the time goes in v4:
time: 326 us; the launch traced here: 320 us
  Pallas kernels  234 us (72%)
  local copies, waits for them, and re-layouts  30.3 us (9%)
  other arithmetic  28.9 us (9%)
  starting transfers between devices  18.3 us (6%)
  waiting for transfers between devices  8.15 us (2%)
    pallas_call x4, Pallas kernels, exchange(): pl.pallas_call(functools.partial(exchange_kernel, reduces, finishes), out...  234 us
    gather x3, local copies, waits for them, and re-layouts, shards(): outgoing = jnp.take(volume_flat, trace_send, axis=0, mode='clip')  16.9 us
    another operation x8, other arithmetic  11.5 us
    all_to_all x3, starting transfers between devices, shards(): lax.all_to_all(outgoing, 'row', split_axis=0, concat_axis=0, tiled=True)  11.2 us
    all_to_all x3, waiting for transfers between devices, shards(): lax.all_to_all(outgoing, 'row', split_axis=0, concat_axis=0, tiled=True)  8.14 us
    ppermute x3, starting transfers between devices, passed_along(): return lax.ppermute(block, axis, route)  7.07 us
  transfers between devices with their start and end apart: 6, of which 2 were waited for; matrix products, arithmetic and copies ran while one was open for 15% of the time, Pallas kernels for 10%

profile of v4, /device:TPU:0, one launch (start us, length us, event | category | flops | bytes accessed | tf_op | source)
XLA Modules:
  0.0 320.5 jit_solution(17124526285581899366)
XLA Ops:
  0.6 1.1 slice.41
  1.8 3.1 collective-permute-start
  6.2 1.6 reduce.12
  7.9 1.6 reduce.13
  9.6 1.0 compare_convert_fusion
  10.6 1.2 reduce-window.26
  12.9 5.7 %gather_fusion = f32[1024,128]{1,0:T(8,128)} fusion(f32[4096,128]{1,0:T(8,128)} %bitcast.58, s32[1024]{0:T(1024)S(1)} %broadcast_clamp_fusion), kind=kCustom, calls=%fused_computation | custom fusion | bytes 1052672 | tf_op jit(solution)/shard_map/jit(_take)/gather | solution.py:399
  18.5 4.0 %all-to-all-start = ((f32[4,256,128]{2,1,0:T(8,128)}), f32[4,256,128]{2,1,0:T(8,128)S(1)}, u32[]{:S(2)}, u32[]{:S(2)}) async-start(f32[4,256,128]{2,1,0:T(8,128)} %bitcast.3), calls=%async_computation | async-start | bytes 1048576 | tf_op jit(solution)/shard_map/all_to_all | solution.py:400
  22.8 4.5 %reduce-window.30 = s32[4,8,4,128]{3,1,2,0:T(8,128)S(1)} reduce-window(s32[4,8,4,128]{3,1,2,0:T(8,128)S(1)} %compare_convert_fusion.3, s32[]{:T(128)} %constant.16.clone.1), window={size=1x1x1x128 pad=0_0x0_0x0_0x127_0}, to_apply=%region_3.4 | reduce-window | flops 2080768 | bytes 131076 | tf_op jit(solution)/shard_map/reduce-window.2
  29.4 4.5 %reduce-window.34 = s32[8,4,4,128]{3,0,1,2:T(8,128)S(1)} reduce-window(s32[8,4,4,128]{3,0,1,2:T(8,128)S(1)} %compare_convert_fusion.2, s32[]{:T(128)} %constant.16.clone.1), window={size=1x1x1x128 pad=0_0x0_0x0_0x127_0}, to_apply=%region_7.8 | reduce-window | flops 2080768 | bytes 131076 | tf_op jit(solution)/shard_map/reduce-window.4
  34.3 1.2 reduce-window.36
  37.2 32.4 %shard_map.122 = (f32[512,128]{1,0:T(8,128)S(1)}, f32[4,512,128]{2,1,0:T(8,128)S(1)}) custom-call(f32[512,128]{1,0:T(8,128)S(1)} %constant_dynamic-slice_fusion.2.refs_0_), custom_call_target="tpu_custom_call" | custom-call | flops 1000 | bytes 150000000 | tf_op jit(solution)/shard_map/pallas_call | solution.py:311
  72.4 1.0 reduce-precision_convert_fusion.8
  73.7 68.6 %shard_map.123 = (f32[8,512,128]{2,1,0:T(8,128)}, f32[512,128]{1,0:T(8,128)S(1)}, f32[4,512,128]{2,1,0:T(8,128)S(1)}) custom-call(bf16[2048,256]{1,0:T(8,128)(2,1)S(1)} %pad_maximum_fusion.refs_0_, bf16[8,128,256]{2,1,0:T(8,128)(2,1)S(1)} %pad_maximum_fusion.3.refs_1_, s32[8,1,128]{2,1,0:T(1,128)S(1)} %reshape.216.refs_2_, f32[4096,2048]{1,0:T(8,128)} %refs_3_.5, ...), custom_call_target="tpu_custom_call" | custom-call | flops 1000 | bytes 150000000 | tf_op jit(solution)/shard_map/pallas_call | solution.py:311
  143.2 1.7 slice.42
  144.9 2.0 collective-permute-start.1
  146.9 5.6 %gather_fusion.1 = f32[1024,128]{1,0:T(8,128)} fusion(f32[4096,128]{1,0:T(8,128)} %bitcast.60, s32[1024]{0:T(1024)S(1)} %broadcast_clamp_fusion), kind=kCustom, calls=%fused_computation.1 | custom fusion | bytes 1052672 | tf_op jit(solution)/shard_map/jit(_take)/gather | solution.py:399
  152.5 3.5 %all-to-all-start.1 = ((f32[4,256,128]{2,1,0:T(8,128)}), f32[4,256,128]{2,1,0:T(8,128)S(1)}, u32[]{:S(2)}, u32[]{:S(2)}) async-start(f32[4,256,128]{2,1,0:T(8,128)} %bitcast.16), calls=%async_computation.1 | async-start | bytes 1048576 | tf_op jit(solution)/shard_map/all_to_all | solution.py:400
  156.0 1.2 pad_maximum_fusion.1.refs_0_
  157.3 1.0 reduce-precision_convert_fusion.7
  158.3 4.2 %all-to-all-done.1 = f32[4,256,128]{2,1,0:T(8,128)S(1)} async-done(((f32[4,256,128]{2,1,0:T(8,128)}), f32[4,256,128]{2,1,0:T(8,128)S(1)}, u32[]{:S(2)}, u32[]{:S(2)}) %all-to-all-start.1) | async-done | bytes 524320 | tf_op jit(solution)/shard_map/all_to_all | solution.py:400
  162.7 70.4 %shard_map.124 = (f32[8,512,128]{2,1,0:T(8,128)}, f32[512,128]{1,0:T(8,128)S(1)}, f32[4,512,128]{2,1,0:T(8,128)S(1)}) custom-call(bf16[2048,256]{1,0:T(8,128)(2,1)S(1)} %pad_maximum_fusion.1.refs_0_, bf16[8,128,256]{2,1,0:T(8,128)(2,1)S(1)} %pad_maximum_fusion.4.refs_1_, s32[8,1,128]{2,1,0:T(1,128)S(1)} %reshape.216.refs_2_, f32[4096,2048]{1,0:T(8,128)} %refs_3_.5, ...), custom_call_target="tpu_custom_call" | custom-call | flops 1000 | bytes 150000000 | tf_op jit(solution)/shard_map/pallas_call | solution.py:311
  234.1 1.7 slice.43
  235.8 2.0 collective-permute-start.2
  237.8 5.6 %gather_fusion.2 = f32[1024,128]{1,0:T(8,128)} fusion(f32[4096,128]{1,0:T(8,128)} %bitcast.59, s32[1024]{0:T(1024)S(1)} %broadcast_clamp_fusion), kind=kCustom, calls=%fused_computation.2 | custom fusion | bytes 1052672 | tf_op jit(solution)/shard_map/jit(_take)/gather | solution.py:399
  243.4 3.7 %all-to-all-start.2 = ((f32[4,256,128]{2,1,0:T(8,128)}), f32[4,256,128]{2,1,0:T(8,128)S(1)}, u32[]{:S(2)}, u32[]{:S(2)}) async-start(f32[4,256,128]{2,1,0:T(8,128)} %bitcast.22), calls=%async_computation.2 | async-start | bytes 1048576 | tf_op jit(solution)/shard_map/all_to_all | solution.py:400
  247.2 1.2 pad_maximum_fusion.2.refs_0_
  248.5 1.0 reduce-precision_convert_fusion.6
  249.5 4.0 %all-to-all-done.2 = f32[4,256,128]{2,1,0:T(8,128)S(1)} async-done(((f32[4,256,128]{2,1,0:T(8,128)}), f32[4,256,128]{2,1,0:T(8,128)S(1)}, u32[]{:S(2)}, u32[]{:S(2)}) %all-to-all-start.2) | async-done | bytes 524320 | tf_op jit(solution)/shard_map/all_to_all | solution.py:400
  253.7 62.2 %shard_map.125 = (f32[8,512,128]{2,1,0:T(8,128)S(1)}, f32[8,512,128]{2,1,0:T(8,128)}) custom-call(bf16[2048,256]{1,0:T(8,128)(2,1)S(1)} %pad_maximum_fusion.2.refs_0_, bf16[8,128,256]{2,1,0:T(8,128)(2,1)S(1)} %pad_maximum_fusion.5.refs_1_, s32[8,1,128]{2,1,0:T(1,128)S(1)} %reshape.216.refs_2_, f32[4096,2048]{1,0:T(8,128)} %refs_3_.5, ...), custom_call_target="tpu_custom_call" | custom-call | flops 1000 | bytes 150000000 | tf_op jit(solution)/shard_map/pallas_call | solution.py:311
  315.9 3.2 copy.60
  319.1 1.3 copy.61
  (91 shorter events, 12.4 us)
Async XLA Ops:
  0.6 36.5 %copy-start = (f32[4096,128]{1,0:T(8,128)S(1)}, f32[4096,128]{1,0:T(8,128)}, u32[]{:S(2)}) copy-start(f32[4096,128]{1,0:T(8,128)} %param.11) | copy-start | bytes 6291460
  1.8 70.6 %collective-permute-start = (f32[8,64,128]{2,1,0:T(8,128)S(1)}, f32[8,64,128]{2,1,0:T(8,128)}, u32[]{:S(2)}, u32[]{:S(2)}) collective-permute-start(f32[8,64,128]{2,1,0:T(8,128)S(1)} %slice.41), channel_id=1, source_target_pairs={{0,1},{1,2},{2,3},{3,4},{4,5},{5,6},{6,7},{7,8},{8,9},{9,10},{10,1... | collective-permute-start | bytes 786440 | tf_op jit(solution)/shard_map/ppermute | solution.py:21
  12.9 16.3 %copy-start.3 = (s32[16384]{0:T(1024)S(1)}, s32[16384]{0:T(1024)}, u32[]{:S(2)}) copy-start(s32[16384]{0:T(1024)} %param.20) | copy-start | bytes 196612
  18.5 54.9 %all-to-all-start = ((f32[4,256,128]{2,1,0:T(8,128)}), f32[4,256,128]{2,1,0:T(8,128)S(1)}, u32[]{:S(2)}, u32[]{:S(2)}) async-start(f32[4,256,128]{2,1,0:T(8,128)} %bitcast.3), calls=%async_computation | async-start | bytes 1048576 | tf_op jit(solution)/shard_map/all_to_all | solution.py:400
  69.6 1.0 copy-start.2
  69.6 0.9 copy-start.4
  69.8 1.9 copy-start.5
  144.9 12.4 %collective-permute-start.1 = (f32[8,64,128]{2,1,0:T(8,128)}, f32[8,64,128]{2,1,0:T(8,128)}, u32[]{:S(2)}, u32[]{:S(2)}) collective-permute-start(f32[8,64,128]{2,1,0:T(8,128)} %slice.42), channel_id=1, source_target_pairs={{0,1},{1,2},{2,3},{3,4},{4,5},{5,6},{6,7},{7,8},{8,9},{9,10},{10,1... | collective-permute-start | bytes 786440 | tf_op jit(solution)/shard_map/ppermute | solution.py:21
  152.5 10.0 %all-to-all-start.1 = ((f32[4,256,128]{2,1,0:T(8,128)}), f32[4,256,128]{2,1,0:T(8,128)S(1)}, u32[]{:S(2)}, u32[]{:S(2)}) async-start(f32[4,256,128]{2,1,0:T(8,128)} %bitcast.16), calls=%async_computation.1 | async-start | bytes 1048576 | tf_op jit(solution)/shard_map/all_to_all | solution.py:400
  235.8 12.7 %collective-permute-start.2 = (f32[8,64,128]{2,1,0:T(8,128)}, f32[8,64,128]{2,1,0:T(8,128)}, u32[]{:S(2)}, u32[]{:S(2)}) collective-permute-start(f32[8,64,128]{2,1,0:T(8,128)} %slice.43), channel_id=1, source_target_pairs={{0,1},{1,2},{2,3},{3,4},{4,5},{5,6},{6,7},{7,8},{8,9},{9,10},{10,1... | collective-permute-start | bytes 786440 | tf_op jit(solution)/shard_map/ppermute | solution.py:21
  243.4 10.1 %all-to-all-start.2 = ((f32[4,256,128]{2,1,0:T(8,128)}), f32[4,256,128]{2,1,0:T(8,128)S(1)}, u32[]{:S(2)}, u32[]{:S(2)}) async-start(f32[4,256,128]{2,1,0:T(8,128)} %bitcast.22), calls=%async_computation.2 | async-start | bytes 1048576 | tf_op jit(solution)/shard_map/all_to_all | solution.py:400
  315.9 4.5 %copy-start.1 = (f32[4096,128]{1,0:T(8,128)S(1)}, f32[4096,128]{1,0:T(8,128)}, u32[]{:S(2)}) copy-start(f32[4096,128]{1,0:T(8,128)} %param.11) | copy-start | bytes 6291460
